TPU v7x, 128 devices: a whole 4x4x4 slice. The times are simulated.
128 devices in a mesh: dev: 128 (over y, z, x, core).
Axes of the slice: x: 4, y: 4, z: 4, core: 2. Of those that a mesh axis runs over, the one named last changes fastest.
Arguments:
- gaussians: float32 [59, 1048576], P(None, 'dev'), may hold values from -6 to 3
- view_angles: float32 [3], replicated, may hold values from -4 to 4
- tile_order: int32 [2048], P('dev'), may hold values from 0 to 2047, as said below
- tile_owners: int32 [2048, 512], P('dev'), may hold values from 0 to 127, as said below
- tile_locals: int32 [2048, 512], P('dev'), may hold values from 0 to 8191
- list_counts: int32 [2048], P('dev'), may hold values from 1 to 512, as said below
- image_cotangent: float32 [3, 524288], P(None, 'dev'), may hold values from -6 to 6
Outputs:
- rendered: float32 [3, 524288], P(None, 'dev')
- gradients: float32 [59, 1048576], P(None, 'dev')
Inputs may be any that keep to these rules, and one draw needn't show every extreme that they name: `tile_order`: each image tile once. `tile_owners`: the 16 x 512 slots of the tiles of one device name every owner exactly 64 times. Slots from list_counts[i] on are padding.
All inputs are finite; a program needn't handle non-finite values.
Results may differ from a plain program's by a relative error of at most 0.0003.
Values sent between devices are 32-bit elements; how exact they have to be, the bound alone decides.
A program may use at most 64 MiB of HBM per device.

v0:
```python
from functools import partial

import jax
import jax.numpy as jnp
from jax import lax
from jax.sharding import PartitionSpec as P

PIX = 256
TX = 32
SLOTS = 512
BLOCK = 256


highest = lax.Precision.HIGHEST


def rotation_of(view_angles):
    cos_a = jnp.cos(view_angles[0])
    sin_a = jnp.sin(view_angles[0])
    cos_b = jnp.cos(view_angles[1])
    sin_b = jnp.sin(view_angles[1])
    cos_c = jnp.cos(view_angles[2])
    sin_c = jnp.sin(view_angles[2])
    zero_val = jnp.zeros((), jnp.float32)
    one_val = jnp.ones((), jnp.float32)
    turn_x = jnp.stack(
        [
            jnp.stack([one_val, zero_val, zero_val]),
            jnp.stack([zero_val, cos_a, -sin_a]),
            jnp.stack([zero_val, sin_a, cos_a]),
        ]
    )
    turn_y = jnp.stack(
        [
            jnp.stack([cos_b, zero_val, sin_b]),
            jnp.stack([zero_val, one_val, zero_val]),
            jnp.stack([-sin_b, zero_val, cos_b]),
        ]
    )
    turn_z = jnp.stack(
        [
            jnp.stack([cos_c, -sin_c, zero_val]),
            jnp.stack([sin_c, cos_c, zero_val]),
            jnp.stack([zero_val, zero_val, one_val]),
        ]
    )
    return jnp.dot(turn_z, jnp.dot(turn_y, turn_x, precision=highest), precision=highest)


def harmonics(along_x, along_y, along_z):
    sq_x = along_x * along_x
    sq_y = along_y * along_y
    sq_z = along_z * along_z
    return jnp.stack(
        [
            0.28209479177387814 + 0.0 * along_x,
            -0.4886025119029199 * along_y,
            0.4886025119029199 * along_z,
            -0.4886025119029199 * along_x,
            1.0925484305920792 * along_x * along_y,
            -1.0925484305920792 * along_y * along_z,
            0.31539156525252005 * (2.0 * sq_z - sq_x - sq_y),
            -1.0925484305920792 * along_x * along_z,
            0.5462742152960396 * (sq_x - sq_y),
            -0.5900435899266435 * along_y * (3.0 * sq_x - sq_y),
            2.890611442640554 * along_x * along_y * along_z,
            -0.4570457994644658 * along_y * (4.0 * sq_z - sq_x - sq_y),
            0.3731763325901154 * along_z * (2.0 * sq_z - 3.0 * sq_x - 3.0 * sq_y),
            -0.4570457994644658 * along_x * (4.0 * sq_z - sq_x - sq_y),
            1.445305721320277 * along_z * (sq_x - sq_y),
            -0.5900435899266435 * along_x * (sq_x - 3.0 * sq_y),
        ]
    )


def project(columns, view_angles, camera_frame):
    focal_x, focal_y, centre_x, centre_y = camera_frame
    rotation = rotation_of(view_angles)
    positions = columns[0:3]
    cam_first = (
        rotation[0, 0] * positions[0]
        + rotation[0, 1] * positions[1]
        + rotation[0, 2] * positions[2]
    )
    cam_second = (
        rotation[1, 0] * positions[0]
        + rotation[1, 1] * positions[1]
        + rotation[1, 2] * positions[2]
    )
    mean_x = centre_x + focal_x * cam_first
    mean_y = centre_y + focal_y * cam_second
    scales = jnp.exp(columns[3:6])
    quat_w = columns[6]
    quat_x = columns[7]
    quat_y = columns[8]
    quat_z = columns[9]
    norm_sq = jnp.maximum(
        quat_w * quat_w + quat_x * quat_x + quat_y * quat_y + quat_z * quat_z, 1.0
    )
    turned = [
        [
            1.0 - 2.0 * (quat_y * quat_y + quat_z * quat_z) / norm_sq,
            2.0 * (quat_x * quat_y - quat_w * quat_z) / norm_sq,
            2.0 * (quat_x * quat_z + quat_w * quat_y) / norm_sq,
        ],
        [
            2.0 * (quat_x * quat_y + quat_w * quat_z) / norm_sq,
            1.0 - 2.0 * (quat_x * quat_x + quat_z * quat_z) / norm_sq,
            2.0 * (quat_y * quat_z - quat_w * quat_x) / norm_sq,
        ],
        [
            2.0 * (quat_x * quat_z - quat_w * quat_y) / norm_sq,
            2.0 * (quat_y * quat_z + quat_w * quat_x) / norm_sq,
            1.0 - 2.0 * (quat_x * quat_x + quat_y * quat_y) / norm_sq,
        ],
    ]
    first_row = []
    second_row = []
    for column_index in range(3):
        first_row.append(
            focal_x
            * (
                rotation[0, 0] * turned[0][column_index]
                + rotation[0, 1] * turned[1][column_index]
                + rotation[0, 2] * turned[2][column_index]
            )
            * scales[column_index]
        )
        second_row.append(
            focal_y
            * (
                rotation[1, 0] * turned[0][column_index]
                + rotation[1, 1] * turned[1][column_index]
                + rotation[1, 2] * turned[2][column_index]
            )
            * scales[column_index]
        )
    cov_a = (
        first_row[0] * first_row[0]
        + first_row[1] * first_row[1]
        + first_row[2] * first_row[2]
        + 0.3
    )
    cov_b = (
        first_row[0] * second_row[0] + first_row[1] * second_row[1] + first_row[2] * second_row[2]
    )
    cov_c = (
        second_row[0] * second_row[0]
        + second_row[1] * second_row[1]
        + second_row[2] * second_row[2]
        + 0.3
    )
    determinant = cov_a * cov_c - cov_b * cov_b
    opacity = 1.0 / (1.0 + jnp.exp(-columns[10]))
    basis = harmonics(rotation[2, 0], rotation[2, 1], rotation[2, 2])
    coeffs = columns[11:59].reshape(3, 16, columns.shape[1])
    colours = 0.5 + jnp.einsum("k,ckn->cn", basis, coeffs, precision=highest)
    return jnp.stack(
        [
            mean_x,
            mean_y,
            cov_c / determinant,
            -cov_b / determinant,
            cov_a / determinant,
            opacity,
            colours[0],
            colours[1],
            colours[2],
        ]
    )


def render_tile(tile_rows, live_count, tile_id):
    pixels = jnp.arange(PIX, dtype=jnp.int32)
    pixel_x = (tile_id % TX * 16 + pixels % 16).astype(jnp.float32) + 0.5
    pixel_y = (tile_id // TX * 16 + pixels // 16).astype(jnp.float32) + 0.5
    before = (jnp.arange(BLOCK)[:, None] < jnp.arange(BLOCK)[None, :]).astype(jnp.float32)

    def one_block(start, state):
        log_carry, tile_image = state
        segment = tile_rows[:, start : start + BLOCK]
        offset_x = pixel_x[:, None] - segment[0][None, :]
        offset_y = pixel_y[:, None] - segment[1][None, :]
        powers = (
            -0.5
            * (
                segment[2][None, :] * offset_x * offset_x
                + segment[4][None, :] * offset_y * offset_y
            )
            - segment[3][None, :] * offset_x * offset_y
        )
        slot_live = start + jnp.arange(BLOCK, dtype=jnp.int32) < live_count
        alphas = jnp.where(slot_live[None, :], segment[5][None, :] * jnp.exp(powers), 0.0)
        logs = jnp.log1p(-alphas)
        summed = log_carry[:, None] + jnp.dot(logs, before, precision=highest)
        weights = jnp.exp(summed) * alphas
        added = jnp.einsum("ck,pk->cp", segment[6:9], weights, precision=highest)
        return (log_carry + jnp.sum(logs, axis=1), tile_image + added)

    state = (jnp.zeros((PIX,), jnp.float32), jnp.zeros((3, PIX), jnp.float32))
    for block_index in range(SLOTS // BLOCK):
        start = block_index * BLOCK
        step_block = partial(one_block, start)
        if block_index == 0:
            state = step_block(state)
        else:
            state = step_block(state)
    return state[1]


def shards(
    gaussians, view_angles, tile_order, tile_owners, tile_locals, list_counts, image_cotangent
):
    devices = lax.axis_size("dev")
    tile_count = tile_order.shape[0]
    tiles_y = devices * tile_count // TX
    camera_frame = (4.0 * TX, 4.0 * tiles_y, 8.0 * TX, 8.0 * tiles_y)
    owner_flat = tile_owners.reshape(-1)
    local_flat = tile_locals.reshape(-1)
    slot_total = owner_flat.shape[0]
    per_owner = slot_total // devices
    grouping = jnp.argsort(owner_flat, stable=True)
    inverse = (
        jnp.zeros((slot_total,), jnp.int32)
        .at[grouping]
        .set(jnp.arange(slot_total, dtype=jnp.int32))
    )
    wanted = jnp.take(local_flat, grouping).reshape(devices, per_owner)

    def shade_tile(columns, live_count, tile_id):
        return render_tile(project(columns, view_angles, camera_frame), live_count, tile_id)

    asked = lax.all_to_all(wanted, "dev", split_axis=0, concat_axis=0, tiled=True)
    picked = jnp.take(gaussians, asked.reshape(-1), axis=0 + 1).reshape(
        gaussians.shape[0], asked.shape[0], asked.shape[1]
    )
    arrived = lax.all_to_all(picked, "dev", split_axis=1, concat_axis=1, tiled=True)
    asked_ids = asked[None]
    row_width = arrived.shape[0]
    slot_rows = jnp.take(arrived.reshape(row_width, slot_total), inverse, axis=1)
    tile_rows = slot_rows.reshape(row_width, tile_count, SLOTS).transpose(1, 0, 2)
    cotangents = image_cotangent.reshape(3, tile_count, PIX).transpose(1, 0, 2)

    def one_tile(tile_item):
        columns, live_count, tile_id, tile_cot = tile_item
        tile_image, pullback = jax.vjp(
            lambda values: shade_tile(values, live_count, tile_id), columns
        )
        return (tile_image, pullback(tile_cot)[0])

    images, slot_grads = lax.map(one_tile, (tile_rows, list_counts, tile_order, cotangents))
    rendered = images.transpose(1, 0, 2).reshape(3, tile_count * PIX)
    grouped = jnp.take(
        slot_grads.transpose(1, 0, 2).reshape(row_width, slot_total), grouping, axis=1
    )
    received = asked_ids.reshape(slot_total)
    terms = lax.all_to_all(grouped, "dev", split_axis=1, concat_axis=1, tiled=True)
    gradients = jnp.zeros_like(gaussians).at[:, received].add(terms)
    return (rendered, gradients)


def solution(mesh):
    return jax.shard_map(
        shards,
        mesh=mesh,
        in_specs=(
            P(None, "dev"),
            P(),
            P("dev"),
            P("dev", None),
            P("dev", None),
            P("dev"),
            P(None, "dev"),
        ),
        out_specs=(P(None, "dev"), P(None, "dev")),
        check_vma=False,
    )
```

profile of v0, /device:TPU:1, one launch (start us, length us, event | category | flops | bytes accessed | tf_op | source)
XLA Modules:
  0.0 779.5 jit_solution(3245866421442171446)
XLA Ops:
  1.4 6.8 sort.17
  9.0 45.5 %gather_fusion = s32[8192]{0:T(1024)S(1)} fusion(s32[8192]{0:T(1024)S(1)} %bitcast.294, s32[8192]{0:T(1024)S(1)} %get-tuple-element.583), kind=kCustom, calls=%fused_computation.3 | custom fusion | bytes 98304 | tf_op jit(solution)/shard_map/jit(_take)/gather | solution.py:228
  55.3 11.5 %all-to-all-start = ((s32[128,1,64]{2,1,0:T(1,128)}), s32[128,1,64]{2,1,0:T(1,128)S(1)}, u32[]{:S(2)}, u32[]{:S(2)}) async-start(s32[128,1,64]{2,1,0:T(1,128)} %bitcast.51), calls=%async_computation | async-start | bytes 131072 | tf_op jit(solution)/shard_map/all_to_all | solution.py:233
  66.8 2.8 copy.20
  69.5 6.6 all-to-all-done
  77.6 29.9 %gather_fusion.1 = f32[8192,59]{1,0:T(8,128)} fusion(f32[59,8192]{0,1:T(8,128)} %copy.20, s32[8192]{0:T(1024)S(1)} %fusion.144), kind=kCustom, calls=%fused_computation.clone | custom fusion | bytes 3899392 | tf_op jit(solution)/shard_map/jit(_take)/gather | solution.py:234
  107.5 7.5 broadcast_select_fusion.2
  115.0 8.0 %reshape.1740 = f32[128,1,3776]{2,1,0:T(1,128)} reshape(f32[128,64,59]{2,1,0:T(8,128)} %bitcast.297) | data formatting | bytes 3866624
  123.0 4.6 all-to-all-start.1
  153.9 30.7 %scatter_custom_fusion = s32[8192]{0:T(1024)S(1)} fusion(s32[8192]{0:T(1024)S(1)} %get-tuple-element.582, s32[8192]{0:T(1024)S(1)} %iota.61, s32[]{:T(128)} %constant.284.clone.1), kind=kCustom, calls=%fused_computation.308 | custom fusion | bytes 32772 | tf_op jit(solution)/shard_map/scatter | solution.py:226
  185.4 7.1 reduce.6
  192.5 8.2 %reshape.1741 = f32[128,64,59]{2,1,0:T(8,128)} reshape(f32[128,3776]{1,0:T(8,128)} %reduce.6) | data formatting | bytes 3866624
  200.7 29.9 %gather_fusion.2 = f32[8192,59]{1,0:T(8,128)} fusion(f32[59,8192]{0,1:T(8,128)} %bitcast.295, s32[8192]{0:T(1024)S(1)} %fusion.145), kind=kCustom, calls=%fused_computation.1.clone | custom fusion | bytes 3899392 | tf_op jit(solution)/shard_map/jit(_take)/gather | solution.py:240
  230.6 7.5 broadcast_select_fusion.1
  238.1 2.9 copy.21
  241.0 375.3 %while.15 = (s32[]{:T(128)}, f32[16,3,256]{2,1,0:T(4,128)S(1)}, f32[16,59,512]{2,1,0:T(8,128)}, f32[16,59,512]{2,1,0:T(8,128)S(1)}, f32[16]{0:T(128)S(1)}, /*ind...) while((s32[]{:T(128)}, f32[16,3,256]{2,1,0:T(4,128)S(1)}, ...), condition=%wide.region_17.19_spmd, body=%wide.region_2.18_spmd.sunk | while | flops 835476480 | bytes 4493020 | solution.py:251
  241.8 3.8 fusion.262
  248.6 3.8 add_bitcast_fusion.3
  255.5 1.1 fusion.276
  265.3 3.8 fusion.262
  272.0 3.8 add_bitcast_fusion.3
  279.0 1.1 fusion.276
  288.7 3.8 fusion.262
  295.5 3.8 add_bitcast_fusion.3
  306.1 1.1 fusion.275
  312.2 3.8 fusion.262
  318.9 3.8 add_bitcast_fusion.3
  335.7 3.8 fusion.262
  342.4 3.8 add_bitcast_fusion.3
  359.1 3.8 fusion.262
  365.8 3.8 add_bitcast_fusion.3
  372.8 1.1 fusion.276
  382.6 3.8 fusion.262
  389.3 3.8 add_bitcast_fusion.3
  399.9 1.1 fusion.275
  406.0 3.8 fusion.262
  412.8 3.8 add_bitcast_fusion.3
  423.4 1.1 fusion.275
  429.5 3.8 fusion.262
  436.2 3.8 add_bitcast_fusion.3
  453.0 3.8 fusion.262
  459.7 3.8 add_bitcast_fusion.3
  476.4 3.8 fusion.262
  483.2 3.8 add_bitcast_fusion.3
  499.9 3.8 fusion.262
  506.6 3.8 add_bitcast_fusion.3
  523.4 3.8 fusion.262
  530.1 3.8 add_bitcast_fusion.3
  546.8 3.8 fusion.262
  553.5 3.8 add_bitcast_fusion.3
  570.3 3.8 fusion.262
  577.0 3.8 add_bitcast_fusion.3
  593.7 3.8 fusion.262
  600.5 3.8 add_bitcast_fusion.3
  616.4 3.9 copy.23
  620.3 29.9 %gather_fusion.3 = f32[8192,59]{1,0:T(8,128)} fusion(f32[59,8192]{0,1:T(8,128)} %bitcast.296, s32[8192]{0:T(1024)S(1)} %get-tuple-element.583), kind=kCustom, calls=%fused_computation.2.clone | custom fusion | bytes 3899392 | tf_op jit(solution)/shard_map/jit(_take)/gather | solution.py:253
  650.2 7.5 broadcast_select_fusion
  657.7 17.1 %reshape.1742 = f32[128,1,3776]{2,1,0:T(1,128)} reshape(f32[128,64,59]{2,1,0:T(8,128)} %bitcast.299) | data formatting | bytes 3866624
  674.8 9.8 %all-to-all-start.2 = ((f32[128,1,3776]{2,1,0:T(1,128)}), f32[128,1,3776]{2,1,0:T(1,128)S(1)}, u32[]{:S(2)}, u32[]{:S(2)}) async-start(f32[128,1,3776]{2,1,0:T(1,128)} %reshape.1742), calls=%async_computation.2 | async-start | bytes 3932160 | tf_op jit(solution)/shard_map/all_to_all | solution.py:257
  684.7 29.0 %all-to-all-done.2 = f32[128,1,3776]{2,1,0:T(1,128)S(1)} async-done(((f32[128,1,3776]{2,1,0:T(1,128)}), f32[128,1,3776]{2,1,0:T(1,128)S(1)}, u32[]{:S(2)}, u32[]{:S(2)}) %all-to-all-start.2) | async-done | bytes 1933344 | tf_op jit(solution)/shard_map/all_to_all | solution.py:257
  713.7 7.1 reduce.7
  720.8 8.2 %reshape.1743 = f32[128,64,59]{2,1,0:T(8,128)} reshape(f32[128,3776]{1,0:T(8,128)} %reduce.7) | data formatting | bytes 3866624
  729.0 46.5 %scatter_custom_fusion.1 = f32[59,8192]{0,1:T(8,128)} fusion(s32[8192]{0:T(1024)S(1)} %bitcast.313, f32[8192,59]{1,0:T(8,128)} %bitcast.302, f32[]{:T(128)} %constant.285.clone.1), kind=kCustom, calls=%fused_computation.295 | custom fusion | flops 483328 | bytes 1933824 | tf_op jit(solution)/shard_map/scatter-add | solution.py:258
  775.5 3.8 copy.24
  (902 shorter events, 212.6 us)
Async XLA Ops:
  9.0 57.8 %copy-start = (f32[59,8192]{1,0:T(8,128)S(1)}, f32[59,8192]{1,0:T(8,128)}, u32[]{:S(2)}) copy-start(f32[59,8192]{1,0:T(8,128)} %param.11) | copy-start | bytes 5799940
  55.3 20.9 %all-to-all-start = ((s32[128,1,64]{2,1,0:T(1,128)}), s32[128,1,64]{2,1,0:T(1,128)S(1)}, u32[]{:S(2)}, u32[]{:S(2)}) async-start(s32[128,1,64]{2,1,0:T(1,128)} %bitcast.51), calls=%async_computation | async-start | bytes 131072 | tf_op jit(solution)/shard_map/all_to_all | solution.py:233
  115.0 12.6 %copy-start.1 = (f32[3]{0:T(128)S(1)}, f32[3]{0:T(128)}, u32[]{:S(2)}) copy-start(f32[3]{0:T(128)} %param.12) | copy-start | bytes 40
  115.0 17.7 %copy-start.6 = (f32[1,3]{1,0:T(1,128)S(1)}, f32[1,3]{1,0:T(1,128)}, u32[]{:S(2)}) copy-start(f32[1,3]{1,0:T(1,128)} %constant.291.clone.1) | copy-start | bytes 40
  115.0 17.7 %copy-start.7 = (f32[1,3]{1,0:T(1,128)S(1)}, f32[1,3]{1,0:T(1,128)}, u32[]{:S(2)}) copy-start(f32[1,3]{1,0:T(1,128)} %constant.292.clone.1) | copy-start | bytes 40
  115.0 17.9 %copy-start.2 = (f32[1,3]{1,0:T(1,128)S(1)}, f32[1,3]{1,0:T(1,128)}, u32[]{:S(2)}) copy-start(f32[1,3]{1,0:T(1,128)} %constant.290.clone.1) | copy-start | bytes 40
  123.0 61.8 %all-to-all-start.1 = ((f32[128,1,3776]{2,1,0:T(1,128)}), f32[128,1,3776]{2,1,0:T(1,128)S(1)}, u32[]{:S(2)}, u32[]{:S(2)}) async-start(f32[128,1,3776]{2,1,0:T(1,128)} %reshape.1740), calls=%async_computation.1 | async-start | bytes 3932160 | tf_op jit(solution)/shard_map/all_to_all | solution.py:237
  238.1 2.9 copy-start.3
  238.1 3.0 copy-start.4
  616.4 33.8 %copy-start.5 = (f32[16,3,256]{2,1,0:T(4,128)}, f32[16,3,256]{2,1,0:T(4,128)S(1)}, u32[]{:S(2)}) copy-start(f32[16,3,256]{2,1,0:T(4,128)S(1)} %get-tuple-element.419) | copy-start | bytes 147460
  674.8 38.9 %all-to-all-start.2 = ((f32[128,1,3776]{2,1,0:T(1,128)}), f32[128,1,3776]{2,1,0:T(1,128)S(1)}, u32[]{:S(2)}, u32[]{:S(2)}) async-start(f32[128,1,3776]{2,1,0:T(1,128)} %reshape.1742), calls=%async_computation.2 | async-start | bytes 3932160 | tf_op jit(solution)/shard_map/all_to_all | solution.py:257
where the time goes:
time: 794 us; the launch traced here: 780 us
  other arithmetic  262 us (33%)
  local copies, waits for them, and re-layouts  257 us (32%)
  matrix products  131 us (16%)
  loops' own time  41.8 us (5%)
  waiting for transfers between devices  35.7 us (4%)
  starting transfers between devices  25.9 us (3%)
  between operations  25.5 us (3%)
    dot_general x96, matrix products, one_block(): added = jnp.einsum('ck,pk->cp', segment[6:9], weights, precision=highest)  85.6 us
    div x16, other arithmetic, project(): cov_c / determinant  60.5 us
    add x16, other arithmetic, project(): mean_x = centre_x + focal_x * cam_first  60.1 us
    unnamed x24, local copies, waits for them, and re-layouts  49.8 us
    scatter-add x1, other arithmetic, shards(): gradients = jnp.zeros_like(gaussians).at[:, received].add(terms)  46.5 us
    gather x1, local copies, waits for them, and re-layouts, shards(): wanted = jnp.take(local_flat, grouping).reshape(devices, per_owner)  45.5 us
    dot_general x64, matrix products, one_block(): summed = log_carry[:, None] + jnp.dot(logs, before, precision=highest)  42.2 us
    another operation x1, loops' own time, shards(): lax.map(one_tile, (tile_rows, list_counts, tile_order, cotangents))  41.8 us
  transfers between devices with their start and end apart: 3, of which 2 were waited for; matrix products, arithmetic and copies ran while one was open for 5% of the time, Pallas kernels for 0%

commit v1 on v0

v1 whole, which is shorter than its diff:
```python
from functools import partial

import jax
import jax.numpy as jnp
from jax import lax
from jax.experimental import pallas as pl
from jax.experimental.pallas import tpu as pltpu
from jax.sharding import PartitionSpec as P

DEVS = 128
CHIPS = 64
TILES = 16
SLOTS = 512
ROWS = 64
LANES = 128
PROJ = 9
PIX = 256
TX = 32
FOCAL_X = 128.0
FOCAL_Y = 256.0
CENTRE_X = 256.0
CENTRE_Y = 512.0
LOG2E = 1.4426950408889634
MESH = pl.DeviceIdType.MESH
f32 = jnp.float32
bf16 = jnp.bfloat16
i32 = jnp.int32


def iota(shape, dim):
    return lax.broadcasted_iota(i32, shape, dim)


def split2(x):
    hi = x.astype(bf16)
    return hi, (x - hi.astype(f32)).astype(bf16)


def split3(x):
    hi = x.astype(bf16)
    rest = x - hi.astype(f32)
    mid = rest.astype(bf16)
    return hi, mid, (rest - mid.astype(f32)).astype(bf16)


def lane_pick(table, index):
    return jnp.take_along_axis(table, index, axis=1)


def view_of(angle_ref):
    def turn(i):
        angle = jnp.full((8, LANES), angle_ref[i], f32)
        return jnp.cos(angle)[0:1], jnp.sin(angle)[0:1]

    (ca, sa), (cb, sb), (cc, sc) = turn(0), turn(1), turn(2)
    first = (cc * cb, cc * sb * sa - sc * ca, cc * sb * ca + sc * sa)
    second = (sc * cb, sc * sb * sa + cc * ca, sc * sb * ca - cc * sa)
    third = (-sb, cb * sa, cb * ca)
    return first, second, third


def harmonics(x, y, z):
    xx, yy, zz = x * x, y * y, z * z
    return [
        0.28209479177387814 + 0.0 * x,
        -0.4886025119029199 * y,
        0.4886025119029199 * z,
        -0.4886025119029199 * x,
        1.0925484305920792 * x * y,
        -1.0925484305920792 * y * z,
        0.31539156525252005 * (2.0 * zz - xx - yy),
        -1.0925484305920792 * x * z,
        0.5462742152960396 * (xx - yy),
        -0.5900435899266435 * y * (3.0 * xx - yy),
        2.890611442640554 * x * y * z,
        -0.4570457994644658 * y * (4.0 * zz - xx - yy),
        0.3731763325901154 * z * (2.0 * zz - 3.0 * xx - 3.0 * yy),
        -0.4570457994644658 * x * (4.0 * zz - xx - yy),
        1.445305721320277 * z * (xx - yy),
        -0.5900435899266435 * x * (xx - 3.0 * yy),
    ]


COLOUR_ROWS = ((8, 32), (24, 48), (40, 59))


def colour_weights(basis):
    out = []
    for c, (low, high) in enumerate(COLOUR_ROWS):
        row = iota((high - low, LANES), 0) + low - (11 + 16 * c)
        held = jnp.zeros((high - low, LANES), f32)
        for k in range(16):
            held = jnp.where(row == k, basis[k], held)
        out.append(held)
    return out


def project(params, first, second):
    px, py, pz, s0, s1, s2, qw, qx, qy, qz, logit = params
    mean_x = CENTRE_X + FOCAL_X * (first[0] * px + first[1] * py + first[2] * pz)
    mean_y = CENTRE_Y + FOCAL_Y * (second[0] * px + second[1] * py + second[2] * pz)
    scales = (jnp.exp(s0), jnp.exp(s1), jnp.exp(s2))
    two_n = 2.0 / jnp.maximum(qw * qw + qx * qx + qy * qy + qz * qz, 1.0)
    turned = (
        (1.0 - two_n * (qy * qy + qz * qz), two_n * (qx * qy - qw * qz), two_n * (qx * qz + qw * qy)),
        (two_n * (qx * qy + qw * qz), 1.0 - two_n * (qx * qx + qz * qz), two_n * (qy * qz - qw * qx)),
        (two_n * (qx * qz - qw * qy), two_n * (qy * qz + qw * qx), 1.0 - two_n * (qx * qx + qy * qy)),
    )
    va = []
    vb = []
    for j in range(3):
        va.append(FOCAL_X * (first[0] * turned[0][j] + first[1] * turned[1][j] + first[2] * turned[2][j]) * scales[j])
        vb.append(FOCAL_Y * (second[0] * turned[0][j] + second[1] * turned[1][j] + second[2] * turned[2][j]) * scales[j])
    cov_a = va[0] * va[0] + va[1] * va[1] + va[2] * va[2] + 0.3
    cov_b = va[0] * vb[0] + va[1] * vb[1] + va[2] * vb[2]
    cov_c = vb[0] * vb[0] + vb[1] * vb[1] + vb[2] * vb[2] + 0.3
    inv = 1.0 / (cov_a * cov_c - cov_b * cov_b)
    log_opacity = -jnp.log(1.0 + jnp.exp(-logit))
    return mean_x, mean_y, cov_c * inv, -cov_b * inv, cov_a * inv, log_opacity


def regroup(table_ref, rows_of, index, store):
    part_rows = 32
    for part in range(ROWS // part_rows):
        flat = index[part * part_rows : (part + 1) * part_rows]
        high = lax.shift_right_logical(flat, 7)
        low = jnp.bitwise_and(flat, 127)

        def step(i, held):
            here = high == i
            out = []
            for r in range(PROJ):
                row = jnp.broadcast_to(table_ref[r, pl.ds(i, 1), :], (part_rows, LANES))
                out.append(jnp.where(here, lane_pick(row, low), held[r]))
            return tuple(out)

        start = tuple(jnp.zeros((part_rows, LANES), f32) for _ in range(PROJ))
        taken = lax.fori_loop(0, ROWS, step, start, unroll=2)
        for r in range(PROJ):
            store(r, part * part_rows, taken[r])


def chain_length(count):
    return lax.shift_left(lax.shift_right_logical(count + 31, 5), 2)


def route_kernel(count_ref, owner_ref, local_ref, want_ref, pos_ref, group_ref, own_s, loc_s, carry_s, sum_s):
    tile = iota((TILES, LANES), 0)
    length = jnp.zeros((TILES, LANES), i32)
    for t in range(TILES):
        length = jnp.where(tile == t, chain_length(count_ref[t]), length)
    for d in range(SLOTS // LANES):
        row = iota((TILES, LANES), 1) + d * LANES
        slot = jnp.where(row < 8 * length, jnp.bitwise_and(row, 7) * length + lax.shift_right_logical(row, 3), row)
        high = lax.shift_right_logical(slot, 7)
        low = jnp.bitwise_and(slot, 127)
        for src, dst in ((owner_ref, own_s), (local_ref, loc_s)):
            held = jnp.zeros((TILES, LANES), i32)
            for c in range(SLOTS // LANES):
                held = jnp.where(high == c, lane_pick(src[:, c * LANES : (c + 1) * LANES], low), held)
            dst[:, d * LANES : (d + 1) * LANES] = held
    half = 256
    before = jnp.where(iota((half, half), 0) < iota((half, half), 1), 1.0, 0.0).astype(bf16)
    ones = jnp.ones((half, half), bf16)
    both = jnp.concatenate([before, ones], axis=1)
    carry_s[...] = jnp.zeros_like(carry_s)
    sum_s[...] = jnp.zeros_like(sum_s)
    owner_id = iota((DEVS, half), 0)
    pair_id = iota((ROWS, half), 0)
    lane_id = iota((LANES, half), 0)

    def step(t, _):
        for h in range(2):
            owner = own_s[pl.ds(t, 1), h * half : (h + 1) * half]
            local = loc_s[pl.ds(t, 1), h * half : (h + 1) * half]
            hit = owner_id == owner
            hit_f = jnp.where(hit, 1.0, 0.0)
            counts = jnp.dot(hit_f.astype(bf16), both, preferred_element_type=f32)
            seen = carry_s[...]
            rank = jnp.sum(hit_f * (counts[:, :half] + seen), axis=0, keepdims=True).astype(i32)
            carry_s[...] = seen + counts[:, half:]
            place = owner * ROWS + rank
            pos_ref[pl.ds(4 * t + 2 * h, 1), :] = place[:, :LANES]
            pos_ref[pl.ds(4 * t + 2 * h + 1, 1), :] = place[:, LANES:]
            pair = pair_id == lax.shift_right_logical(place, 7)
            lane = jnp.where(lane_id == jnp.bitwise_and(place, 127), 1.0, 0.0).astype(bf16)
            slot = t * SLOTS + h * half + iota((1, half), 1)
            parts = []
            for number in (local, slot):
                for part in (lax.shift_right_logical(number, 7), jnp.bitwise_and(number, 127)):
                    parts.append(jnp.where(pair, part.astype(f32), 0.0).astype(bf16))
            sum_s[...] += lax.dot_general(
                jnp.concatenate(parts, axis=0), lane, (((1,), (1,)), ((), ())), preferred_element_type=f32
            )
        return 0

    lax.fori_loop(0, TILES, step, 0)
    total = sum_s[...].astype(i32)
    want_ref[:, 0, :] = total[0:64] * 128 + total[64:128]
    group_ref[...] = total[128:192] * 128 + total[192:256]


def exchange_kernel(x_ref, y_ref, near, far, send_sem, recv_sem, pair_sem):
    me = lax.axis_index("dev")
    chip = me // 2
    core = me % 2
    other = chip * 2 + (1 - core)
    barrier = pltpu.get_barrier_semaphore()

    def greet(i, _):
        peer = ((chip + i) % CHIPS) * 2 + core
        pl.semaphore_signal(barrier, inc=1, device_id=(peer,), device_id_type=MESH)
        return 0

    lax.fori_loop(1, CHIPS, greet, 0)
    pl.semaphore_signal(barrier, inc=1, device_id=(other,), device_id_type=MESH)
    pl.semaphore_wait(barrier, CHIPS)

    def outgoing(i):
        to = (chip + i) % CHIPS
        return pltpu.make_async_remote_copy(
            src_ref=x_ref.at[to],
            dst_ref=near.at[chip],
            send_sem=send_sem.at[i],
            recv_sem=recv_sem.at[i],
            device_id=(to * 2 + core,),
            device_id_type=MESH,
        )

    def incoming(i):
        source = (chip + CHIPS - i) % CHIPS
        return pltpu.make_async_remote_copy(
            src_ref=x_ref.at[source],
            dst_ref=near.at[source],
            send_sem=send_sem.at[i],
            recv_sem=recv_sem.at[i],
            device_id=(source * 2 + core,),
            device_id_type=MESH,
        )

    def send(i, _):
        outgoing(i).start()
        return 0

    lax.fori_loop(1, CHIPS, send, 0)
    near[chip] = x_ref[chip]

    def receive(i, _):
        incoming(i).wait_recv()
        return 0

    lax.fori_loop(1, CHIPS, receive, 0)
    swap = pltpu.make_async_remote_copy(
        src_ref=near,
        dst_ref=far,
        send_sem=pair_sem.at[0],
        recv_sem=pair_sem.at[1],
        device_id=(other,),
        device_id_type=MESH,
    )
    swap.start()

    def sent(i, _):
        outgoing(i).wait_send()
        return 0

    lax.fori_loop(1, CHIPS, sent, 0)
    swap.wait()
    shape = (CHIPS, LANES)
    mine = lax.shift_right_logical(iota(shape, 1), 6) == core
    for r in range(x_ref.shape[1]):
        y_ref[:, r, :] = jnp.where(mine, near[:, r, :], pltpu.roll(far[:, r, :], 64, 1))


def exchange(x, number):
    vmem = pl.BlockSpec(memory_space=pltpu.VMEM)
    return pl.pallas_call(
        exchange_kernel,
        out_shape=jax.ShapeDtypeStruct(x.shape, x.dtype),
        in_specs=[vmem],
        out_specs=vmem,
        scratch_shapes=[
            pltpu.VMEM(x.shape, x.dtype),
            pltpu.VMEM(x.shape, x.dtype),
            pltpu.SemaphoreType.DMA((CHIPS,)),
            pltpu.SemaphoreType.DMA((CHIPS,)),
            pltpu.SemaphoreType.DMA((2,)),
        ],
        compiler_params=pltpu.CompilerParams(collective_id=number, has_side_effects=True),
        name="exchange_" + str(number),
    )(x)


def spread(gauss_ref, held, row_of):
    for i in range(ROWS):
        at = row_of(i) * 16
        held[at : at + 16, :] = gauss_ref[0:16, i * LANES : (i + 1) * LANES]
    return [held[pl.ds(r, ROWS, stride=16), :] for r in range(11)]


def answer_kernel(angle_ref, gauss_ref, asked_ref, out_ref, held, table):
    first, second, third = view_of(angle_ref)
    weights = colour_weights(harmonics(*third))
    params = spread(gauss_ref, held, lambda i: i)
    for r, value in enumerate(project(params, first, second)):
        table[r] = value
    for i in range(ROWS):
        lanes = slice(i * LANES, (i + 1) * LANES)
        for c, (low, high) in enumerate(COLOUR_ROWS):
            table[6 + c, i : i + 1, :] = 0.5 + jnp.sum(
                gauss_ref[low:high, lanes] * weights[c], axis=0, keepdims=True
            )

    def store(r, at, value):
        out_ref[at : at + value.shape[0], r, :] = value

    regroup(table, ROWS, asked_ref[:, 0, :], store)


def render_kernel(
    count_ref, order_ref, got_ref, pos_ref, group_ref, cot_ref, image_ref, grad_ref,
    table, where_s, coef, sums, alpha_s, w_s, v_s, gh_s, gl_s, wh_s, wl_s,
):
    shape = (ROWS, LANES)
    tile = lax.shift_right_logical(iota(shape, 0), 2)
    row = jnp.bitwise_and(iota(shape, 0), 3) * LANES + iota(shape, 1)
    length = jnp.zeros(shape, i32)
    count = jnp.zeros(shape, i32)
    shown = jnp.zeros(shape, i32)
    for t in range(TILES):
        here = tile == t
        length = jnp.where(here, chain_length(count_ref[t]), length)
        count = jnp.where(here, count_ref[t], count)
        shown = jnp.where(here, order_ref[t], shown)
    slot = jnp.where(row < 8 * length, jnp.bitwise_and(row, 7) * length + lax.shift_right_logical(row, 3), row)
    live = slot < count
    mid_x = (jnp.bitwise_and(shown, TX - 1) * 16 + 8).astype(f32)
    mid_y = (lax.shift_right_logical(shown, 5) * 16 + 8).astype(f32)

    for r in range(PROJ):
        table[r] = got_ref[:, r, :]

    def keep(r, at, value):
        where_s[r, at : at + value.shape[0], :] = value

    regroup(table, ROWS, pos_ref[...], keep)
    mx = where_s[0] - mid_x
    my = where_s[1] - mid_y
    ca, cb, cc = where_s[2], where_s[3], where_s[4]
    where_s[0] = mx
    where_s[1] = my
    numbers = (
        LOG2E * (-0.5 * (ca * mx * mx + cc * my * my) - cb * mx * my + where_s[5]),
        LOG2E * (ca * mx + cb * my),
        LOG2E * (cc * my + cb * mx),
        (-0.5 * LOG2E) * ca,
        -LOG2E * cb,
        (-0.5 * LOG2E) * cc,
        where_s[6],
        where_s[7],
        where_s[8],
    )
    coef[...] = jnp.zeros_like(coef)
    for q, number in enumerate(numbers):
        coef[pl.ds(q, ROWS, stride=16), :] = jnp.where(live, number, -1e9 if q == 0 else 0.0)
    wh_s[...] = jnp.zeros_like(wh_s)
    wl_s[...] = jnp.zeros_like(wl_s)
    gh_s[...] = jnp.zeros_like(gh_s)
    gl_s[...] = jnp.zeros_like(gl_s)

    flat = (16, PIX)
    line = iota(flat, 0)
    ox = jnp.bitwise_and(iota(flat, 1), 15).astype(f32) - 7.5
    oy = lax.shift_right_logical(iota(flat, 1), 4).astype(f32) - 7.5
    terms = (jnp.ones(flat, f32), ox, oy, ox * ox, ox * oy, oy * oy)
    basis = jnp.zeros(flat, f32)
    for q, term in enumerate(terms):
        basis = jnp.where(line == q, term, basis)
    basis = basis.astype(bf16)
    none = jnp.zeros(flat, bf16)
    powers_rhs = jnp.concatenate([basis, basis, basis, none, none, none], axis=0)
    sub = iota((8, PIX), 0)
    contract_first = (((0,), (0,)), ((), ()))
    contract_last = (((1,), (1,)), ((), ()))

    def one_tile(t, _):
        parts = []
        for c in range(4):
            at = pl.multiple_of((4 * t + c) * 16, 16)
            parts.append(coef[pl.ds(at, 16), :])
        hi, mid, lo = split3(jnp.concatenate(parts, axis=1))
        at = pl.multiple_of(t * PIX, PIX)
        cot = jnp.zeros(flat, f32)
        for c in range(3):
            cot = jnp.where(line == 6 + c, cot_ref[c : c + 1, pl.ds(at, PIX)], cot)
        t_hi, t_mid, t_lo = split3(cot)
        lhs = jnp.concatenate([hi, mid, lo, hi, mid, hi], axis=0)
        cot_rhs = jnp.concatenate([t_hi, t_hi, t_hi, t_mid, t_mid, t_lo], axis=0)
        alpha_s[...] = jnp.exp2(lax.dot_general(lhs, powers_rhs, contract_first, preferred_element_type=f32))
        w_s[...] = lax.dot_general(lhs, cot_rhs, contract_first, preferred_element_type=f32)
        blocks = lax.shift_right_logical(chain_length(count_ref[t]), 2)

        def forward(b, state):
            left, total = state
            base = pl.multiple_of(b * 32, 32)
            for j in range(4):
                rows = pl.ds(base + 8 * j, 8)
                v = left * alpha_s[rows, :]
                v_s[rows, :] = v
                left = left - v
                total = total + v * w_s[rows, :]
            return left, total

        left, total = lax.fori_loop(
            0, blocks, forward, (jnp.ones((8, PIX), f32), jnp.zeros((8, PIX), f32))
        )
        enter = jnp.ones((8, PIX), f32)
        run = left[0:1]
        for s in range(1, 8):
            enter = jnp.where(sub == s, run, enter)
            run = run * left[s : s + 1]
        behind = jnp.zeros((8, PIX), f32)
        run = total[7:8]
        for s in range(6, -1, -1):
            behind = jnp.where(sub == s, run, behind)
            run = total[s : s + 1] + left[s : s + 1] * run

        def backward(i, behind):
            base = pl.multiple_of((blocks - 1 - i) * 32, 32)
            weights = [None] * 4
            grads = [None] * 4
            for j in range(3, -1, -1):
                rows = pl.ds(base + 8 * j, 8)
                gap = w_s[rows, :] - behind
                weights[j] = enter * v_s[rows, :]
                grads[j] = weights[j] * gap
                behind = behind + alpha_s[rows, :] * gap
            rows = pl.ds(base, 32)
            wh_s[rows, :], wl_s[rows, :] = split2(jnp.concatenate(weights, axis=0))
            gh_s[rows, :], gl_s[rows, :] = split2(jnp.concatenate(grads, axis=0))
            return behind

        lax.fori_loop(0, blocks, backward, behind)
        wh, wl = wh_s[...], wl_s[...]

        def pixel_sum(a, b):
            return lax.dot_general(a, b, contract_last, preferred_element_type=f32)

        got = (
            pixel_sum(basis, gh_s[...])
            + pixel_sum(basis, gl_s[...])
            + pixel_sum(t_hi, wh)
            + pixel_sum(t_mid, wh)
            + pixel_sum(t_hi, wl)
        )
        for c in range(4):
            at_c = pl.multiple_of((4 * t + c) * 16, 16)
            sums[pl.ds(at_c, 16), :] = got[:, c * LANES : (c + 1) * LANES]
        image = (
            jnp.dot(hi, wh, preferred_element_type=f32)
            + jnp.dot(mid, wh, preferred_element_type=f32)
            + jnp.dot(hi, wl, preferred_element_type=f32)
        )
        image_ref[:, pl.ds(at, PIX)] = image[6:9]
        return 0

    lax.fori_loop(0, TILES, one_tile, 0)

    s = [sums[pl.ds(q, ROWS, stride=16), :] for q in range(PROJ)]
    mx, my, ca, cb, cc = (where_s[r] for r in range(5))
    sx = s[1] - mx * s[0]
    sy = s[2] - my * s[0]
    grads = (
        ca * sx + cb * sy,
        cc * sy + cb * sx,
        -0.5 * (s[3] - mx * (s[1] + sx)),
        -(s[4] - mx * s[2] - my * sx),
        -0.5 * (s[5] - my * (s[2] + sy)),
        s[0],
        s[6],
        s[7],
        s[8],
    )
    for r in range(PROJ):
        table[r] = jnp.where(live, grads[r], 0.0)

    def hand(r, at, value):
        grad_ref[at : at + value.shape[0], r, :] = value

    regroup(table, ROWS, group_ref[...], hand)


def pull_kernel(angle_ref, gauss_ref, asked_ref, got_ref, out_ref, held, acc, back):
    first, second, third = view_of(angle_ref)
    weights = colour_weights(harmonics(*third))
    acc[...] = jnp.zeros_like(acc)
    high_id = iota((32, PIX), 0)
    low_id = iota((PIX, PIX), 0)

    def add(i, _):
        index = jnp.concatenate([asked_ref[2 * i], asked_ref[2 * i + 1]], axis=1)
        here = high_id == lax.shift_right_logical(index, 8)
        low = jnp.where(low_id == jnp.bitwise_and(index, 255), 1.0, 0.0).astype(bf16)
        value = jnp.concatenate([got_ref[2 * i], got_ref[2 * i + 1]], axis=1)
        hi = value.astype(bf16).astype(f32)
        lo = value - hi
        rows = []
        for r in range(PROJ):
            for part in (hi, lo):
                rows.append(jnp.where(here, part[r : r + 1], 0.0).astype(bf16))
        acc[...] += lax.dot_general(
            jnp.concatenate(rows, axis=0), low, (((1,), (1,)), ((), ())), preferred_element_type=f32
        )
        return 0

    lax.fori_loop(0, ROWS // 2, add, 0)
    slot_sum = []
    for r in range(PROJ):
        both = acc[64 * r : 64 * r + 32, :] + acc[64 * r + 32 : 64 * r + 64, :]
        slot_sum.append(jnp.concatenate([both[:, :LANES], both[:, LANES:]], axis=0))

    def row_of(i):
        return (i % 2) * 32 + i // 2

    params = spread(gauss_ref, held, row_of)
    _, pullback = jax.vjp(lambda *p: project(p, first, second), *params)
    grads = pullback(tuple(slot_sum[:6]))
    held[...] = jnp.zeros_like(held)
    for r in range(11):
        held[pl.ds(r, ROWS, stride=16), :] = grads[r]
    for c in range(3):
        back[c] = slot_sum[6 + c]
    for i in range(ROWS):
        at = row_of(i)
        lanes = slice(i * LANES, (i + 1) * LANES)
        tint = [back[c, at : at + 1, :] for c in range(3)]
        w0, w1, w2 = weights
        out_ref[0:8, lanes] = held[at * 16 : at * 16 + 8, :]
        out_ref[8:16, lanes] = held[at * 16 + 8 : at * 16 + 16, :] + w0[0:8] * tint[0]
        out_ref[16:24, lanes] = w0[8:16] * tint[0]
        out_ref[24:32, lanes] = w0[16:24] * tint[0] + w1[0:8] * tint[1]
        out_ref[32:40, lanes] = w1[8:16] * tint[1]
        out_ref[40:48, lanes] = w1[16:24] * tint[1] + w2[0:8] * tint[2]
        out_ref[48:56, lanes] = w2[8:16] * tint[2]
        out_ref[56:59, lanes] = w2[16:19] * tint[2]


VMEM = pl.BlockSpec(memory_space=pltpu.VMEM)
SMEM = pl.BlockSpec(memory_space=pltpu.SMEM)


def sds(shape, dtype=f32):
    return jax.ShapeDtypeStruct(shape, dtype)


def route(counts, owners, locals_):
    return pl.pallas_call(
        route_kernel,
        out_shape=(sds((ROWS, 1, LANES), i32), sds((ROWS, LANES), i32), sds((ROWS, LANES), i32)),
        in_specs=[SMEM, VMEM, VMEM],
        out_specs=(VMEM, VMEM, VMEM),
        scratch_shapes=[
            pltpu.VMEM((TILES, SLOTS), i32),
            pltpu.VMEM((TILES, SLOTS), i32),
            pltpu.VMEM((DEVS, 256), f32),
            pltpu.VMEM((256, LANES), f32),
        ],
        name="route",
    )(counts, owners, locals_)


def answer(angles, gaussians, asked):
    return pl.pallas_call(
        answer_kernel,
        out_shape=sds((ROWS, PROJ, LANES)),
        in_specs=[SMEM, VMEM, VMEM],
        out_specs=VMEM,
        scratch_shapes=[pltpu.VMEM((ROWS * 16, LANES), f32), pltpu.VMEM((PROJ, ROWS, LANES), f32)],
        name="answer",
    )(angles, gaussians, asked)


def render(counts, order, got, pos, group, cot):
    return pl.pallas_call(
        render_kernel,
        out_shape=(sds((3, TILES * PIX)), sds((ROWS, PROJ, LANES))),
        in_specs=[SMEM, SMEM, VMEM, VMEM, VMEM, VMEM],
        out_specs=(VMEM, VMEM),
        scratch_shapes=[
            pltpu.VMEM((PROJ, ROWS, LANES), f32),
            pltpu.VMEM((PROJ, ROWS, LANES), f32),
            pltpu.VMEM((ROWS * 16, LANES), f32),
            pltpu.VMEM((ROWS * 16, LANES), f32),
            pltpu.VMEM((SLOTS, PIX), f32),
            pltpu.VMEM((SLOTS, PIX), f32),
            pltpu.VMEM((SLOTS, PIX), f32),
            pltpu.VMEM((SLOTS, PIX), bf16),
            pltpu.VMEM((SLOTS, PIX), bf16),
            pltpu.VMEM((SLOTS, PIX), bf16),
            pltpu.VMEM((SLOTS, PIX), bf16),
        ],
        name="render",
    )(counts, order, got, pos, group, cot)


def pull(angles, gaussians, asked, got):
    return pl.pallas_call(
        pull_kernel,
        out_shape=sds(gaussians.shape),
        in_specs=[SMEM, VMEM, VMEM, VMEM],
        out_specs=VMEM,
        scratch_shapes=[
            pltpu.VMEM((ROWS * 16, LANES), f32),
            pltpu.VMEM((64 * PROJ, PIX), f32),
            pltpu.VMEM((3, ROWS, LANES), f32),
        ],
        name="pull",
    )(angles, gaussians, asked, got)


def shards(gaussians, view_angles, tile_order, tile_owners, tile_locals, list_counts, image_cotangent):
    wanted, pos, group = route(list_counts, tile_owners, tile_locals)
    asked = exchange(wanted, 0)
    picked = answer(view_angles, gaussians, asked)
    arrived = exchange(picked, 1)
    rendered, slot_grads = render(list_counts, tile_order, arrived, pos, group, image_cotangent)
    returned = exchange(slot_grads, 2)
    gradients = pull(view_angles, gaussians, asked, returned)
    return rendered, gradients


def solution(mesh):
    return jax.shard_map(
        shards,
        mesh=mesh,
        in_specs=(
            P(None, "dev"),
            P(),
            P("dev"),
            P("dev", None),
            P("dev", None),
            P("dev"),
            P(None, "dev"),
        ),
        out_specs=(P(None, "dev"), P(None, "dev")),
        check_vma=False,
    )
```

time: 794 us -> 160 us (0.20); the launches traced: 780 us -> 160 us
  other arithmetic: 262 us -> 0 us
  local copies, waits for them, and re-layouts: 257 us -> 0 us
  Pallas kernels: 0 us -> 159 us
  matrix products: 131 us -> 0 us
  loops' own time: 41.8 us -> 0 us
  waiting for transfers between devices: 35.7 us -> 0 us
  starting transfers between devices: 25.9 us -> 0 us
  between operations: 25.5 us -> 0.66 us
    pallas_call x0 -> x7, Pallas kernels: none -> 159 us  [the longest x1 62.4 us: render(): pl.pallas_call(render_kernel, out_shape=(sds((3, TILES * PIX)), sds((ROWS...]
    gather x4 -> x0, local copies, waits for them, and re-layouts: 135 us -> none  [the longest x1 45.5 us: shards(): wanted = jnp.take(local_flat, grouping).reshape(devices, per_owner)]
    dot_general x178 -> x0, matrix products: 131 us -> none  [the longest x96 85.6 us: one_block(): added = jnp.einsum('ck,pk->cp', segment[6:9], weights, precision=highest)]
    div x48 -> x0, other arithmetic: 61.2 us -> none  [the longest x16 60.5 us: project(): cov_c / determinant]
    add x64 -> x0, other arithmetic: 60.4 us -> none  [the longest x16 60.1 us: project(): mean_x = centre_x + focal_x * cam_first]
    unnamed x24 -> x0, local copies, waits for them, and re-layouts: 49.8 us -> none
    scatter-add x1 -> x0, other arithmetic: 46.5 us -> none  [shards(): gradients = jnp.zeros_like(gaussians).at[:, received].add(terms)]
    another operation x1 -> x0, loops' own time: 41.8 us -> none  [shards(): lax.map(one_tile, (tile_rows, list_counts, tile_order, cotangents))]
  transfers between devices with their start and end apart: 3 -> 0, of which waited for: 2 -> 0; matrix products, arithmetic and copies ran while one was open for 5% -> 0% of each run, Pallas kernels for 0% -> 0%
where the time goes in v1:
time: 160 us
  Pallas kernels  159 us (99%)
    pallas_call x1, Pallas kernels, render(): pl.pallas_call(render_kernel, out_shape=(sds((3, TILES * PIX)), sds((ROWS...  62.4 us
    pallas_call x3, Pallas kernels, exchange(): pl.pallas_call(exchange_kernel, out_shape=jax.ShapeDtypeStruct(x.shape, x...  52.8 us
    pallas_call x1, Pallas kernels, answer(): pl.pallas_call(answer_kernel, out_shape=sds((ROWS, PROJ, LANES)), in_spec...  21.6 us
    pallas_call x1, Pallas kernels, pull(): pl.pallas_call(pull_kernel, out_shape=sds(gaussians.shape), in_specs=[SME...  12.9 us
    pallas_call x1, Pallas kernels, route(): pl.pallas_call(route_kernel, out_shape=(sds((ROWS, 1, LANES), i32), sds((...  9.47 us

profile of v1, /device:TPU:1, one launch (start us, length us, event | category | flops | bytes accessed | tf_op | source)
XLA Modules:
  0.0 159.9 jit_solution(6440958374922881426)
XLA Ops:
  0.6 9.5 %route.1 = (s32[64,1,128]{2,1,0:T(1,128)}, s32[64,128]{1,0:T(8,128)}, s32[64,128]{1,0:T(8,128)}) custom-call(s32[16]{0:T(128)} %count_ref.3, s32[16,512]{1,0:T(8,128)} %owner_ref.1, s32[16,512]{1,0:T(8,128)} %local_ref.1), custom_call_target="tpu_custom_call" | custom-call | tf_op jit(solution)/shard_map/route/pallas_call | solution.py:557
  10.1 19.0 %exchange_0.1.asked_ref = s32[64,1,128]{2,1,0:T(1,128)} custom-call(s32[64,1,128]{2,1,0:T(1,128)} %get-tuple-element.7.x_ref), custom_call_target="tpu_custom_call" | custom-call | tf_op jit(solution)/shard_map/exchange_0/pallas_call | solution.py:277
  29.1 21.6 %answer.1.x_ref = f32[64,9,128]{2,1,0:T(8,128)} custom-call(f32[3]{0:T(128)} %angle_ref.3, f32[59,8192]{1,0:T(8,128)} %gauss_ref.3, s32[64,1,128]{2,1,0:T(1,128)} %exchange_0.1.asked_ref), custom_call_target="tpu_custom_call" | custom-call | tf_op jit(solution)/shard_map/answer/pallas_call | solution.py:573
  50.7 16.8 %exchange_1.1.got_ref = f32[64,9,128]{2,1,0:T(8,128)} custom-call(f32[64,9,128]{2,1,0:T(8,128)} %answer.1.x_ref), custom_call_target="tpu_custom_call" | custom-call | tf_op jit(solution)/shard_map/exchange_1/pallas_call | solution.py:277
  67.6 62.4 %render.1 = (f32[3,4096]{1,0:T(4,128)}, f32[64,9,128]{2,1,0:T(8,128)}) custom-call(s32[16]{0:T(128)} %count_ref.3, s32[16]{0:T(128)} %order_ref.1, f32[64,9,128]{2,1,0:T(8,128)} %exchange_1.1.got_ref, s32[64,128]{1,0:T(8,128)} %get-tuple-element.8.pos_ref, s32[64,128]{1,0:T(8,128)} %get-tuple-element.9.group_ref, f32[3,4096]{1,0:T(4,128)} %cot_ref.1), custom_call_target="tpu_custom_call" | custom-call | tf_op jit(solution)/shard_map/render/pallas_call | solution.py:584
  130.0 17.0 %exchange_2.1.got_ref = f32[64,9,128]{2,1,0:T(8,128)} custom-call(f32[64,9,128]{2,1,0:T(8,128)} %get-tuple-element.11.x_ref), custom_call_target="tpu_custom_call" | custom-call | tf_op jit(solution)/shard_map/exchange_2/pallas_call | solution.py:277
  147.0 12.9 %pull.1 = f32[59,8192]{1,0:T(8,128)} custom-call(f32[3]{0:T(128)} %angle_ref.3, f32[59,8192]{1,0:T(8,128)} %gauss_ref.3, s32[64,1,128]{2,1,0:T(1,128)} %exchange_0.1.asked_ref, f32[64,9,128]{2,1,0:T(8,128)} %exchange_2.1.got_ref), custom_call_target="tpu_custom_call" | custom-call | tf_op jit(solution)/shard_map/pull/pallas_call | solution.py:607

commit v2 on v1

--- a/solution.py
+++ b/solution.py
@@ -120,7 +120,7 @@
 
 
 def regroup(table_ref, rows_of, index, store):
-    part_rows = 32
+    part_rows = 16
     for part in range(ROWS // part_rows):
         flat = index[part * part_rows : (part + 1) * part_rows]
         high = lax.shift_right_logical(flat, 7)
@@ -135,7 +135,7 @@
             return tuple(out)
 
         start = tuple(jnp.zeros((part_rows, LANES), f32) for _ in range(PROJ))
-        taken = lax.fori_loop(0, ROWS, step, start, unroll=2)
+        taken = lax.fori_loop(0, ROWS, step, start, unroll=16)
         for r in range(PROJ):
             store(r, part * part_rows, taken[r])
 
@@ -144,7 +144,7 @@
     return lax.shift_left(lax.shift_right_logical(count + 31, 5), 2)
 
 
-def route_kernel(count_ref, owner_ref, local_ref, want_ref, pos_ref, group_ref, own_s, loc_s, carry_s, sum_s):
+def route(count_ref, owner_ref, local_ref, want_ref, pos_ref, group_ref, own_s, loc_s, carry_s, sum_s):
     tile = iota((TILES, LANES), 0)
     length = jnp.zeros((TILES, LANES), i32)
     for t in range(TILES):
@@ -200,95 +200,101 @@
     group_ref[...] = total[128:192] * 128 + total[192:256]
 
 
-def exchange_kernel(x_ref, y_ref, near, far, send_sem, recv_sem, pair_sem):
+class Exchange:
+    def __init__(self, x_ref, near, far, send_sem, recv_sem, pair_sem):
+        self.refs = (x_ref, near, far)
+        self.sems = (send_sem, recv_sem, pair_sem)
+        me = lax.axis_index("dev")
+        self.chip = me // 2
+        self.core = me % 2
+        self.other = self.chip * 2 + (1 - self.core)
+
+    def copy(self, i):
+        x_ref, near, _ = self.refs
+        to = (self.chip + i) % CHIPS
+        return pltpu.make_async_remote_copy(
+            src_ref=x_ref.at[to],
+            dst_ref=near.at[self.chip],
+            send_sem=self.sems[0].at[i],
+            recv_sem=self.sems[1].at[i],
+            device_id=(to * 2 + self.core,),
+            device_id_type=MESH,
+        )
+
+    def incoming(self, i):
+        x_ref, near, _ = self.refs
+        source = (self.chip + CHIPS - i) % CHIPS
+        return pltpu.make_async_remote_copy(
+            src_ref=x_ref.at[source],
+            dst_ref=near.at[source],
+            send_sem=self.sems[0].at[i],
+            recv_sem=self.sems[1].at[i],
+            device_id=(source * 2 + self.core,),
+            device_id_type=MESH,
+        )
+
+    def send(self):
+        def one(i, _):
+            self.copy(i).start()
+            return 0
+
+        lax.fori_loop(1, CHIPS, one, 0)
+        self.refs[1][self.chip] = self.refs[0][self.chip]
+
+    def receive(self):
+        _, near, far = self.refs
+
+        def arrived(i, _):
+            self.incoming(i).wait_recv()
+            return 0
+
+        lax.fori_loop(1, CHIPS, arrived, 0)
+        swap = pltpu.make_async_remote_copy(
+            src_ref=near,
+            dst_ref=far,
+            send_sem=self.sems[2].at[0],
+            recv_sem=self.sems[2].at[1],
+            device_id=(self.other,),
+            device_id_type=MESH,
+        )
+        swap.start()
+
+        def sent(i, _):
+            self.copy(i).wait_send()
+            return 0
+
+        lax.fori_loop(1, CHIPS, sent, 0)
+        swap.wait()
+
+    def row(self, r):
+        _, near, far = self.refs
+        mine = lax.shift_right_logical(iota((CHIPS, LANES), 1), 6) == self.core
+        return jnp.where(mine, near[:, r, :], pltpu.roll(far[:, r, :], 64, 1))
+
+
+def greet():
     me = lax.axis_index("dev")
     chip = me // 2
     core = me % 2
-    other = chip * 2 + (1 - core)
     barrier = pltpu.get_barrier_semaphore()
 
-    def greet(i, _):
+    def one(i, _):
         peer = ((chip + i) % CHIPS) * 2 + core
         pl.semaphore_signal(barrier, inc=1, device_id=(peer,), device_id_type=MESH)
         return 0
 
-    lax.fori_loop(1, CHIPS, greet, 0)
-    pl.semaphore_signal(barrier, inc=1, device_id=(other,), device_id_type=MESH)
-    pl.semaphore_wait(barrier, CHIPS)
-
-    def outgoing(i):
-        to = (chip + i) % CHIPS
-        return pltpu.make_async_remote_copy(
-            src_ref=x_ref.at[to],
-            dst_ref=near.at[chip],
-            send_sem=send_sem.at[i],
-            recv_sem=recv_sem.at[i],
-            device_id=(to * 2 + core,),
-            device_id_type=MESH,
-        )
-
-    def incoming(i):
-        source = (chip + CHIPS - i) % CHIPS
-        return pltpu.make_async_remote_copy(
-            src_ref=x_ref.at[source],
-            dst_ref=near.at[source],
-            send_sem=send_sem.at[i],
-            recv_sem=recv_sem.at[i],
-            device_id=(source * 2 + core,),
-            device_id_type=MESH,
-        )
-
-    def send(i, _):
-        outgoing(i).start()
-        return 0
-
-    lax.fori_loop(1, CHIPS, send, 0)
-    near[chip] = x_ref[chip]
-
-    def receive(i, _):
-        incoming(i).wait_recv()
-        return 0
-
-    lax.fori_loop(1, CHIPS, receive, 0)
-    swap = pltpu.make_async_remote_copy(
-        src_ref=near,
-        dst_ref=far,
-        send_sem=pair_sem.at[0],
-        recv_sem=pair_sem.at[1],
-        device_id=(other,),
-        device_id_type=MESH,
-    )
-    swap.start()
-
-    def sent(i, _):
-        outgoing(i).wait_send()
-        return 0
-
-    lax.fori_loop(1, CHIPS, sent, 0)
-    swap.wait()
-    shape = (CHIPS, LANES)
-    mine = lax.shift_right_logical(iota(shape, 1), 6) == core
-    for r in range(x_ref.shape[1]):
-        y_ref[:, r, :] = jnp.where(mine, near[:, r, :], pltpu.roll(far[:, r, :], 64, 1))
-
-
-def exchange(x, number):
-    vmem = pl.BlockSpec(memory_space=pltpu.VMEM)
-    return pl.pallas_call(
-        exchange_kernel,
-        out_shape=jax.ShapeDtypeStruct(x.shape, x.dtype),
-        in_specs=[vmem],
-        out_specs=vmem,
-        scratch_shapes=[
-            pltpu.VMEM(x.shape, x.dtype),
-            pltpu.VMEM(x.shape, x.dtype),
-            pltpu.SemaphoreType.DMA((CHIPS,)),
-            pltpu.SemaphoreType.DMA((CHIPS,)),
-            pltpu.SemaphoreType.DMA((2,)),
-        ],
-        compiler_params=pltpu.CompilerParams(collective_id=number, has_side_effects=True),
-        name="exchange_" + str(number),
-    )(x)
+    lax.fori_loop(1, CHIPS, one, 0)
+    pl.semaphore_signal(barrier, inc=1, device_id=(chip * 2 + (1 - core),), device_id_type=MESH)
+
+
+def met():
+    pl.semaphore_wait(pltpu.get_barrier_semaphore(), CHIPS)
+
+
+def exchange_scratch(rows, dtype):
+    box = pltpu.VMEM((CHIPS, rows, LANES), dtype)
+    sem = pltpu.SemaphoreType.DMA((CHIPS,))
+    return [box, box, box, sem, sem, pltpu.SemaphoreType.DMA((2,))]
 
 
 def spread(gauss_ref, held, row_of):
@@ -298,9 +304,21 @@
     return [held[pl.ds(r, ROWS, stride=16), :] for r in range(11)]
 
 
-def answer_kernel(angle_ref, gauss_ref, asked_ref, out_ref, held, table):
+def fetch_kernel(
+    count_ref, angle_ref, owner_ref, local_ref, gauss_hbm, got_ref, asked_ref, pos_ref, group_ref, *scratch
+):
+    own_s, loc_s, carry_s, sum_s, gauss_ref, held, table, load_sem = scratch[:8]
+    load = pltpu.make_async_copy(gauss_hbm, gauss_ref, load_sem)
+    load.start()
+    greet()
+    ask = Exchange(*scratch[8:14])
+    reply = Exchange(*scratch[14:20])
+    route(count_ref, owner_ref, local_ref, scratch[8], pos_ref, group_ref, own_s, loc_s, carry_s, sum_s)
+    met()
+    ask.send()
     first, second, third = view_of(angle_ref)
     weights = colour_weights(harmonics(*third))
+    load.wait()
     params = spread(gauss_ref, held, lambda i: i)
     for r, value in enumerate(project(params, first, second)):
         table[r] = value
@@ -310,11 +328,19 @@
             table[6 + c, i : i + 1, :] = 0.5 + jnp.sum(
                 gauss_ref[low:high, lanes] * weights[c], axis=0, keepdims=True
             )
+    ask.receive()
+    asked = ask.row(0)
+    asked_ref[...] = asked
+    picked = scratch[14]
 
     def store(r, at, value):
-        out_ref[at : at + value.shape[0], r, :] = value
-
-    regroup(table, ROWS, asked_ref[:, 0, :], store)
+        picked[at : at + value.shape[0], r, :] = value
+
+    regroup(table, ROWS, asked, store)
+    reply.send()
+    reply.receive()
+    for r in range(PROJ):
+        got_ref[r] = reply.row(r)
 
 
 def render_kernel(
@@ -337,13 +363,10 @@
     mid_x = (jnp.bitwise_and(shown, TX - 1) * 16 + 8).astype(f32)
     mid_y = (lax.shift_right_logical(shown, 5) * 16 + 8).astype(f32)
 
-    for r in range(PROJ):
-        table[r] = got_ref[:, r, :]
-
     def keep(r, at, value):
         where_s[r, at : at + value.shape[0], :] = value
 
-    regroup(table, ROWS, pos_ref[...], keep)
+    regroup(got_ref, ROWS, pos_ref[...], keep)
     mx = where_s[0] - mid_x
     my = where_s[1] - mid_y
     ca, cb, cc = where_s[2], where_s[3], where_s[4]
@@ -490,51 +513,72 @@
     regroup(table, ROWS, group_ref[...], hand)
 
 
-def pull_kernel(angle_ref, gauss_ref, asked_ref, got_ref, out_ref, held, acc, back):
-    first, second, third = view_of(angle_ref)
-    weights = colour_weights(harmonics(*third))
+def add_kernel(asked_ref, grad_ref, sum_ref, acc, low_s, *scratch):
+    greet()
+    back = Exchange(grad_ref, *scratch)
+    near, far = scratch[:2]
+    low_id = iota((PIX, PIX), 0)
+    high_id = iota((32, PIX), 0)
+
+    def find(i, _):
+        index = jnp.concatenate([asked_ref[pl.ds(2 * i, 1), :], asked_ref[pl.ds(2 * i + 1, 1), :]], axis=1)
+        at = pl.multiple_of(i * PIX, PIX)
+        low_s[pl.ds(at, PIX), :] = jnp.where(low_id == jnp.bitwise_and(index, 255), 1.0, 0.0).astype(bf16)
+        return 0
+
+    met()
+    back.send()
+    lax.fori_loop(0, ROWS // 2, find, 0)
     acc[...] = jnp.zeros_like(acc)
-    high_id = iota((32, PIX), 0)
-    low_id = iota((PIX, PIX), 0)
+    back.receive()
+    mine = lax.shift_right_logical(iota((PROJ, LANES), 1), 6) == back.core
 
     def add(i, _):
-        index = jnp.concatenate([asked_ref[2 * i], asked_ref[2 * i + 1]], axis=1)
+        index = jnp.concatenate([asked_ref[pl.ds(2 * i, 1), :], asked_ref[pl.ds(2 * i + 1, 1), :]], axis=1)
         here = high_id == lax.shift_right_logical(index, 8)
-        low = jnp.where(low_id == jnp.bitwise_and(index, 255), 1.0, 0.0).astype(bf16)
-        value = jnp.concatenate([got_ref[2 * i], got_ref[2 * i + 1]], axis=1)
+        halves = []
+        for j in range(2):
+            halves.append(jnp.where(mine, near[2 * i + j], pltpu.roll(far[2 * i + j], 64, 1)))
+        value = jnp.concatenate(halves, axis=1)
         hi = value.astype(bf16).astype(f32)
         lo = value - hi
         rows = []
         for r in range(PROJ):
             for part in (hi, lo):
                 rows.append(jnp.where(here, part[r : r + 1], 0.0).astype(bf16))
+        at = pl.multiple_of(i * PIX, PIX)
         acc[...] += lax.dot_general(
-            jnp.concatenate(rows, axis=0), low, (((1,), (1,)), ((), ())), preferred_element_type=f32
+            jnp.concatenate(rows, axis=0),
+            low_s[pl.ds(at, PIX), :],
+            (((1,), (1,)), ((), ())),
+            preferred_element_type=f32,
         )
         return 0
 
     lax.fori_loop(0, ROWS // 2, add, 0)
-    slot_sum = []
     for r in range(PROJ):
         both = acc[64 * r : 64 * r + 32, :] + acc[64 * r + 32 : 64 * r + 64, :]
-        slot_sum.append(jnp.concatenate([both[:, :LANES], both[:, LANES:]], axis=0))
+        sum_ref[r] = jnp.concatenate([both[:, :LANES], both[:, LANES:]], axis=0)
+
+
+def pull_kernel(angle_ref, gauss_ref, sum_ref, out_ref, held):
+    first, second, third = view_of(angle_ref)
+    weights = colour_weights(harmonics(*third))
 
     def row_of(i):
         return (i % 2) * 32 + i // 2
 
     params = spread(gauss_ref, held, row_of)
     _, pullback = jax.vjp(lambda *p: project(p, first, second), *params)
-    grads = pullback(tuple(slot_sum[:6]))
+    grads = pullback(tuple(sum_ref[r] for r in range(6)))
     held[...] = jnp.zeros_like(held)
     for r in range(11):
         held[pl.ds(r, ROWS, stride=16), :] = grads[r]
-    for c in range(3):
-        back[c] = slot_sum[6 + c]
+    w0, w1, w2 = weights
     for i in range(ROWS):
         at = row_of(i)
         lanes = slice(i * LANES, (i + 1) * LANES)
-        tint = [back[c, at : at + 1, :] for c in range(3)]
-        w0, w1, w2 = weights
+        tint = [sum_ref[6 + c, at : at + 1, :] for c in range(3)]
         out_ref[0:8, lanes] = held[at * 16 : at * 16 + 8, :]
         out_ref[8:16, lanes] = held[at * 16 + 8 : at * 16 + 16, :] + w0[0:8] * tint[0]
         out_ref[16:24, lanes] = w0[8:16] * tint[0]
@@ -547,37 +591,35 @@
 
 VMEM = pl.BlockSpec(memory_space=pltpu.VMEM)
 SMEM = pl.BlockSpec(memory_space=pltpu.SMEM)
+ANY = pl.BlockSpec(memory_space=pl.ANY)
 
 
 def sds(shape, dtype=f32):
     return jax.ShapeDtypeStruct(shape, dtype)
 
 
-def route(counts, owners, locals_):
+def fetch(counts, angles, owners, locals_, gaussians):
+    box = sds((ROWS, LANES), i32)
     return pl.pallas_call(
-        route_kernel,
-        out_shape=(sds((ROWS, 1, LANES), i32), sds((ROWS, LANES), i32), sds((ROWS, LANES), i32)),
-        in_specs=[SMEM, VMEM, VMEM],
-        out_specs=(VMEM, VMEM, VMEM),
+        fetch_kernel,
+        out_shape=(sds((PROJ, ROWS, LANES)), box, box, box),
+        in_specs=[SMEM, SMEM, VMEM, VMEM, ANY],
+        out_specs=(VMEM, VMEM, VMEM, VMEM),
         scratch_shapes=[
             pltpu.VMEM((TILES, SLOTS), i32),
             pltpu.VMEM((TILES, SLOTS), i32),
             pltpu.VMEM((DEVS, 256), f32),
             pltpu.VMEM((256, LANES), f32),
-        ],
-        name="route",
-    )(counts, owners, locals_)
-
-
-def answer(angles, gaussians, asked):
-    return pl.pallas_call(
-        answer_kernel,
-        out_shape=sds((ROWS, PROJ, LANES)),
-        in_specs=[SMEM, VMEM, VMEM],
-        out_specs=VMEM,
-        scratch_shapes=[pltpu.VMEM((ROWS * 16, LANES), f32), pltpu.VMEM((PROJ, ROWS, LANES), f32)],
-        name="answer",
-    )(angles, gaussians, asked)
+            pltpu.VMEM(gaussians.shape, f32),
+            pltpu.VMEM((ROWS * 16, LANES), f32),
+            pltpu.VMEM((PROJ, ROWS, LANES), f32),
+            pltpu.SemaphoreType.DMA,
+        ]
+        + exchange_scratch(1, i32)
+        + exchange_scratch(PROJ, f32),
+        compiler_params=pltpu.CompilerParams(collective_id=0, has_side_effects=True),
+        name="fetch",
+    )(counts, angles, owners, locals_, gaussians)
 
 
 def render(counts, order, got, pos, group, cot):
@@ -603,30 +645,34 @@
     )(counts, order, got, pos, group, cot)
 
 
-def pull(angles, gaussians, asked, got):
+def add(asked, grads):
+    return pl.pallas_call(
+        add_kernel,
+        out_shape=sds((PROJ, ROWS, LANES)),
+        in_specs=[VMEM, VMEM],
+        out_specs=VMEM,
+        scratch_shapes=[pltpu.VMEM((64 * PROJ, PIX), f32), pltpu.VMEM((TILES * SLOTS, PIX), bf16)]
+        + exchange_scratch(PROJ, f32)[1:],
+        compiler_params=pltpu.CompilerParams(collective_id=1, has_side_effects=True),
+        name="add",
+    )(asked, grads)
+
+
+def pull(angles, gaussians, sums):
     return pl.pallas_call(
         pull_kernel,
         out_shape=sds(gaussians.shape),
-        in_specs=[SMEM, VMEM, VMEM, VMEM],
+        in_specs=[SMEM, VMEM, VMEM],
         out_specs=VMEM,
-        scratch_shapes=[
-            pltpu.VMEM((ROWS * 16, LANES), f32),
-            pltpu.VMEM((64 * PROJ, PIX), f32),
-            pltpu.VMEM((3, ROWS, LANES), f32),
-        ],
+        scratch_shapes=[pltpu.VMEM((ROWS * 16, LANES), f32)],
         name="pull",
-    )(angles, gaussians, asked, got)
+    )(angles, gaussians, sums)
 
 
 def shards(gaussians, view_angles, tile_order, tile_owners, tile_locals, list_counts, image_cotangent):
-    wanted, pos, group = route(list_counts, tile_owners, tile_locals)
-    asked = exchange(wanted, 0)
-    picked = answer(view_angles, gaussians, asked)
-    arrived = exchange(picked, 1)
-    rendered, slot_grads = render(list_counts, tile_order, arrived, pos, group, image_cotangent)
-    returned = exchange(slot_grads, 2)
-    gradients = pull(view_angles, gaussians, asked, returned)
-    return rendered, gradients
+    got, asked, pos, group = fetch(list_counts, view_angles, tile_owners, tile_locals, gaussians)
+    rendered, slot_grads = render(list_counts, tile_order, got, pos, group, image_cotangent)
+    return rendered, pull(view_angles, gaussians, add(asked, slot_grads))
 
 
 def solution(mesh):

time: 160 us -> 111 us (0.69)
  Pallas kernels: 159 us -> 110 us
    pallas_call x1, Pallas kernels: 62.4 us -> 39.1 us  [render(): pl.pallas_call(render_kernel, out_shape=(sds((3, TILES * PIX)), sds((ROWS...]
    pallas_call x5 -> x2, Pallas kernels: 83.9 us -> 67.4 us  [the longest x1 41.3 us: fetch(): pl.pallas_call(fetch_kernel, out_shape=(sds((PROJ, ROWS, LANES)), box, bo...]
    pallas_call x1, Pallas kernels: 12.9 us -> 3.82 us  [pull(): pl.pallas_call(pull_kernel, out_shape=sds(gaussians.shape), in_specs=[SME...]
where the time goes in v2:
time: 111 us
  Pallas kernels  110 us (99%)
    pallas_call x1, Pallas kernels, fetch(): pl.pallas_call(fetch_kernel, out_shape=(sds((PROJ, ROWS, LANES)), box, bo...  41.3 us
    pallas_call x1, Pallas kernels, render(): pl.pallas_call(render_kernel, out_shape=(sds((3, TILES * PIX)), sds((ROWS...  39.1 us
    pallas_call x1, Pallas kernels, add(): pl.pallas_call(add_kernel, out_shape=sds((PROJ, ROWS, LANES)), in_specs=[...  26.1 us
    pallas_call x1, Pallas kernels, pull(): pl.pallas_call(pull_kernel, out_shape=sds(gaussians.shape), in_specs=[SME...  3.82 us

profile of v2, /device:TPU:1, one launch (start us, length us, event | category | flops | bytes accessed | tf_op | source)
XLA Modules:
  0.0 111.0 jit_solution(13454362021492724299)
XLA Ops:
  0.6 41.3 %fetch.1 = (f32[9,64,128]{2,1,0:T(8,128)}, s32[64,128]{1,0:T(8,128)}, s32[64,128]{1,0:T(8,128)}, s32[64,128]{1,0:T(8,128)}) custom-call(s32[16]{0:T(128)} %count_ref.3, f32[3]{0:T(128)} %angle_ref.3, s32[16,512]{1,0:T(8,128)} %owner_ref.1, s32[16,512]{1,0:T(8,128)} %local_ref.1, f32[59,8192]{1,0:T(8,128)} %gauss_ref.1), custom_call_target="tpu_custom_call" | custom-call | tf_op jit(solution)/shard_map/fetch/pallas_call | solution.py:603
  42.0 39.1 %render.1 = (f32[3,4096]{1,0:T(4,128)}, f32[64,9,128]{2,1,0:T(8,128)}) custom-call(s32[16]{0:T(128)} %count_ref.3, s32[16]{0:T(128)} %order_ref.1, f32[9,64,128]{2,1,0:T(8,128)} %get-tuple-element.8.got_ref, s32[64,128]{1,0:T(8,128)} %get-tuple-element.9.pos_ref, s32[64,128]{1,0:T(8,128)} %get-tuple-element.10.group_ref, f32[3,4096]{1,0:T(4,128)} %cot_ref.1), custom_call_target="tpu_custom_call" | custom-call | tf_op jit(solution)/shard_map/render/pallas_call | solution.py:626
  81.1 26.1 %add.1.sum_ref = f32[9,64,128]{2,1,0:T(8,128)} custom-call(s32[64,128]{1,0:T(8,128)} %get-tuple-element.12.asked_ref, f32[64,9,128]{2,1,0:T(8,128)} %get-tuple-element.13.grad_ref), custom_call_target="tpu_custom_call" | custom-call | tf_op jit(solution)/shard_map/add/pallas_call | solution.py:649
  107.2 3.8 %pull.1 = f32[59,8192]{1,0:T(8,128)} custom-call(f32[3]{0:T(128)} %angle_ref.3, f32[59,8192]{1,0:T(8,128)} %gauss_ref.1, f32[9,64,128]{2,1,0:T(8,128)} %add.1.sum_ref), custom_call_target="tpu_custom_call" | custom-call | tf_op jit(solution)/shard_map/pull/pallas_call | solution.py:662

commit v3 on v2

--- a/solution.py
+++ b/solution.py
@@ -140,18 +140,14 @@
             store(r, part * part_rows, taken[r])
 
 
-def chain_length(count):
-    return lax.shift_left(lax.shift_right_logical(count + 31, 5), 2)
-
-
-def route(count_ref, owner_ref, local_ref, want_ref, pos_ref, group_ref, own_s, loc_s, carry_s, sum_s):
-    tile = iota((TILES, LANES), 0)
-    length = jnp.zeros((TILES, LANES), i32)
-    for t in range(TILES):
-        length = jnp.where(tile == t, chain_length(count_ref[t]), length)
+def slot_of(row):
+    return jnp.bitwise_and(row, 7) * (SLOTS // 8) + lax.shift_right_logical(row, 3)
+
+
+def route(owner_ref, local_ref, want_ref, pos_ref, group_ref, own_s, loc_s, carry_s, sum_s):
     for d in range(SLOTS // LANES):
         row = iota((TILES, LANES), 1) + d * LANES
-        slot = jnp.where(row < 8 * length, jnp.bitwise_and(row, 7) * length + lax.shift_right_logical(row, 3), row)
+        slot = slot_of(row)
         high = lax.shift_right_logical(slot, 7)
         low = jnp.bitwise_and(slot, 127)
         for src, dst in ((owner_ref, own_s), (local_ref, loc_s)):
@@ -304,18 +300,22 @@
     return [held[pl.ds(r, ROWS, stride=16), :] for r in range(11)]
 
 
-def fetch_kernel(
-    count_ref, angle_ref, owner_ref, local_ref, gauss_hbm, got_ref, asked_ref, pos_ref, group_ref, *scratch
+def splat_kernel(
+    count_ref, order_ref, angle_ref, owner_ref, local_ref, cot_ref, gauss_hbm, image_ref, sum_ref,
+    own_s, loc_s, carry_s, sum_s, gauss_ref, held, table, where_s, pos_s, group_s, asked_s, coef, sums,
+    alpha_s, w_s, v_s, gh_s, gl_s, wh_s, wl_s, acc, low_s, load_sem, *boxes,
 ):
-    own_s, loc_s, carry_s, sum_s, gauss_ref, held, table, load_sem = scratch[:8]
     load = pltpu.make_async_copy(gauss_hbm, gauss_ref, load_sem)
     load.start()
     greet()
-    ask = Exchange(*scratch[8:14])
-    reply = Exchange(*scratch[14:20])
-    route(count_ref, owner_ref, local_ref, scratch[8], pos_ref, group_ref, own_s, loc_s, carry_s, sum_s)
+    ask, reply, back = (Exchange(*boxes[6 * n : 6 * n + 6]) for n in range(3))
+    wanted, picked, grad_box = boxes[0], boxes[6], boxes[12]
+    near, far = boxes[13], boxes[14]
+
+    route(owner_ref, local_ref, wanted, pos_s, group_s, own_s, loc_s, carry_s, sum_s)
     met()
     ask.send()
+
     first, second, third = view_of(angle_ref)
     weights = colour_weights(harmonics(*third))
     load.wait()
@@ -328,45 +328,47 @@
             table[6 + c, i : i + 1, :] = 0.5 + jnp.sum(
                 gauss_ref[low:high, lanes] * weights[c], axis=0, keepdims=True
             )
+
     ask.receive()
-    asked = ask.row(0)
-    asked_ref[...] = asked
-    picked = scratch[14]
-
-    def store(r, at, value):
+    asked_s[...] = ask.row(0)
+
+    def answer(r, at, value):
         picked[at : at + value.shape[0], r, :] = value
 
-    regroup(table, ROWS, asked, store)
+    regroup(table, ROWS, asked_s[...], answer)
     reply.send()
-    reply.receive()
-    for r in range(PROJ):
-        got_ref[r] = reply.row(r)
-
-
-def render_kernel(
-    count_ref, order_ref, got_ref, pos_ref, group_ref, cot_ref, image_ref, grad_ref,
-    table, where_s, coef, sums, alpha_s, w_s, v_s, gh_s, gl_s, wh_s, wl_s,
-):
+
+    low_id = iota((PIX, PIX), 0)
+    high_id = iota((32, PIX), 0)
+
+    def find(i, _):
+        index = jnp.concatenate([asked_s[pl.ds(2 * i, 1), :], asked_s[pl.ds(2 * i + 1, 1), :]], axis=1)
+        at = pl.multiple_of(i * PIX, PIX)
+        low_s[pl.ds(at, PIX), :] = jnp.where(low_id == jnp.bitwise_and(index, 255), 1.0, 0.0).astype(bf16)
+        return 0
+
+    lax.fori_loop(0, ROWS // 2, find, 0)
+    acc[...] = jnp.zeros_like(acc)
     shape = (ROWS, LANES)
     tile = lax.shift_right_logical(iota(shape, 0), 2)
-    row = jnp.bitwise_and(iota(shape, 0), 3) * LANES + iota(shape, 1)
-    length = jnp.zeros(shape, i32)
+    slot = slot_of(jnp.bitwise_and(iota(shape, 0), 3) * LANES + iota(shape, 1))
     count = jnp.zeros(shape, i32)
     shown = jnp.zeros(shape, i32)
     for t in range(TILES):
         here = tile == t
-        length = jnp.where(here, chain_length(count_ref[t]), length)
         count = jnp.where(here, count_ref[t], count)
         shown = jnp.where(here, order_ref[t], shown)
-    slot = jnp.where(row < 8 * length, jnp.bitwise_and(row, 7) * length + lax.shift_right_logical(row, 3), row)
     live = slot < count
     mid_x = (jnp.bitwise_and(shown, TX - 1) * 16 + 8).astype(f32)
     mid_y = (lax.shift_right_logical(shown, 5) * 16 + 8).astype(f32)
+    reply.receive()
+    for r in range(PROJ):
+        table[r] = reply.row(r)
 
     def keep(r, at, value):
         where_s[r, at : at + value.shape[0], :] = value
 
-    regroup(got_ref, ROWS, pos_ref[...], keep)
+    regroup(table, ROWS, pos_s[...], keep)
     mx = where_s[0] - mid_x
     my = where_s[1] - mid_y
     ca, cb, cc = where_s[2], where_s[3], where_s[4]
@@ -386,10 +388,6 @@
     coef[...] = jnp.zeros_like(coef)
     for q, number in enumerate(numbers):
         coef[pl.ds(q, ROWS, stride=16), :] = jnp.where(live, number, -1e9 if q == 0 else 0.0)
-    wh_s[...] = jnp.zeros_like(wh_s)
-    wl_s[...] = jnp.zeros_like(wl_s)
-    gh_s[...] = jnp.zeros_like(gh_s)
-    gl_s[...] = jnp.zeros_like(gl_s)
 
     flat = (16, PIX)
     line = iota(flat, 0)
@@ -406,88 +404,94 @@
     contract_first = (((0,), (0,)), ((), ()))
     contract_last = (((1,), (1,)), ((), ()))
 
-    def one_tile(t, _):
-        parts = []
-        for c in range(4):
-            at = pl.multiple_of((4 * t + c) * 16, 16)
-            parts.append(coef[pl.ds(at, 16), :])
-        hi, mid, lo = split3(jnp.concatenate(parts, axis=1))
-        at = pl.multiple_of(t * PIX, PIX)
-        cot = jnp.zeros(flat, f32)
-        for c in range(3):
-            cot = jnp.where(line == 6 + c, cot_ref[c : c + 1, pl.ds(at, PIX)], cot)
-        t_hi, t_mid, t_lo = split3(cot)
-        lhs = jnp.concatenate([hi, mid, lo, hi, mid, hi], axis=0)
-        cot_rhs = jnp.concatenate([t_hi, t_hi, t_hi, t_mid, t_mid, t_lo], axis=0)
-        alpha_s[...] = jnp.exp2(lax.dot_general(lhs, powers_rhs, contract_first, preferred_element_type=f32))
-        w_s[...] = lax.dot_general(lhs, cot_rhs, contract_first, preferred_element_type=f32)
-        blocks = lax.shift_right_logical(chain_length(count_ref[t]), 2)
-
-        def forward(b, state):
-            left, total = state
-            base = pl.multiple_of(b * 32, 32)
-            for j in range(4):
-                rows = pl.ds(base + 8 * j, 8)
-                v = left * alpha_s[rows, :]
-                v_s[rows, :] = v
-                left = left - v
-                total = total + v * w_s[rows, :]
-            return left, total
-
-        left, total = lax.fori_loop(
-            0, blocks, forward, (jnp.ones((8, PIX), f32), jnp.zeros((8, PIX), f32))
-        )
-        enter = jnp.ones((8, PIX), f32)
-        run = left[0:1]
-        for s in range(1, 8):
-            enter = jnp.where(sub == s, run, enter)
-            run = run * left[s : s + 1]
-        behind = jnp.zeros((8, PIX), f32)
-        run = total[7:8]
-        for s in range(6, -1, -1):
-            behind = jnp.where(sub == s, run, behind)
-            run = total[s : s + 1] + left[s : s + 1] * run
-
-        def backward(i, behind):
-            base = pl.multiple_of((blocks - 1 - i) * 32, 32)
-            weights = [None] * 4
-            grads = [None] * 4
-            for j in range(3, -1, -1):
-                rows = pl.ds(base + 8 * j, 8)
-                gap = w_s[rows, :] - behind
-                weights[j] = enter * v_s[rows, :]
-                grads[j] = weights[j] * gap
-                behind = behind + alpha_s[rows, :] * gap
-            rows = pl.ds(base, 32)
-            wh_s[rows, :], wl_s[rows, :] = split2(jnp.concatenate(weights, axis=0))
-            gh_s[rows, :], gl_s[rows, :] = split2(jnp.concatenate(grads, axis=0))
-            return behind
-
-        lax.fori_loop(0, blocks, backward, behind)
-        wh, wl = wh_s[...], wl_s[...]
+    def one_pair(p, _):
+        at, hi, mid, t_hi, t_mid, lhs, cot_rhs = [], [], [], [], [], [], []
+        for u in range(2):
+            t = 2 * p + u
+            parts = []
+            for c in range(4):
+                at_c = pl.multiple_of((4 * t + c) * 16, 16)
+                parts.append(coef[pl.ds(at_c, 16), :])
+            c_hi, c_mid, c_lo = split3(jnp.concatenate(parts, axis=1))
+            at.append(pl.multiple_of(t * PIX, PIX))
+            cot = jnp.zeros(flat, f32)
+            for c in range(3):
+                cot = jnp.where(line == 6 + c, cot_ref[c : c + 1, pl.ds(at[u], PIX)], cot)
+            d_hi, d_mid, d_lo = split3(cot)
+            hi.append(c_hi)
+            mid.append(c_mid)
+            t_hi.append(d_hi)
+            t_mid.append(d_mid)
+            lhs.append(jnp.concatenate([c_hi, c_mid, c_lo, c_hi, c_mid, c_hi], axis=0))
+            cot_rhs.append(jnp.concatenate([d_hi, d_hi, d_hi, d_mid, d_mid, d_lo], axis=0))
+
+        for u in range(2):
+            for b in range(4):
+                part = lhs[u][:, b * 128 : (b + 1) * 128]
+                rows = slice(b * 128, (b + 1) * 128)
+                alpha_s[u, rows] = jnp.exp2(
+                    lax.dot_general(part, powers_rhs, contract_first, preferred_element_type=f32)
+                )
+                w_s[u, rows] = lax.dot_general(part, cot_rhs[u], contract_first, preferred_element_type=f32)
+
+        left = [jnp.ones((8, PIX), f32)] * 2
+        total = [jnp.zeros((8, PIX), f32)] * 2
+        for j in range(SLOTS // 8):
+            rows = slice(8 * j, 8 * j + 8)
+            for u in range(2):
+                v = left[u] * alpha_s[u, rows]
+                v_s[u, rows] = v
+                left[u] = left[u] - v
+                total[u] = total[u] + v * w_s[u, rows]
+        enter, behind = [], []
+        for u in range(2):
+            front = jnp.ones((8, PIX), f32)
+            run = left[u][0:1]
+            for s in range(1, 8):
+                front = jnp.where(sub == s, run, front)
+                run = run * left[u][s : s + 1]
+            enter.append(front)
+            back = jnp.zeros((8, PIX), f32)
+            run = total[u][7:8]
+            for s in range(6, -1, -1):
+                back = jnp.where(sub == s, run, back)
+                run = total[u][s : s + 1] + left[u][s : s + 1] * run
+            behind.append(back)
+        for i in range(SLOTS // 16 - 1, -1, -1):
+            both = slice(16 * i, 16 * i + 16)
+            for u in range(2):
+                weights = [None] * 2
+                grads = [None] * 2
+                for j in (1, 0):
+                    rows = slice(16 * i + 8 * j, 16 * i + 8 * j + 8)
+                    gap = w_s[u, rows] - behind[u]
+                    weights[j] = enter[u] * v_s[u, rows]
+                    grads[j] = weights[j] * gap
+                    behind[u] = behind[u] + alpha_s[u, rows] * gap
+                wh_s[u, both], wl_s[u, both] = split2(jnp.concatenate(weights, axis=0))
+                gh_s[u, both], gl_s[u, both] = split2(jnp.concatenate(grads, axis=0))
 
         def pixel_sum(a, b):
             return lax.dot_general(a, b, contract_last, preferred_element_type=f32)
 
-        got = (
-            pixel_sum(basis, gh_s[...])
-            + pixel_sum(basis, gl_s[...])
-            + pixel_sum(t_hi, wh)
-            + pixel_sum(t_mid, wh)
-            + pixel_sum(t_hi, wl)
-        )
-        for c in range(4):
-            at_c = pl.multiple_of((4 * t + c) * 16, 16)
-            sums[pl.ds(at_c, 16), :] = got[:, c * LANES : (c + 1) * LANES]
-        image = (
-            jnp.dot(hi, wh, preferred_element_type=f32)
-            + jnp.dot(mid, wh, preferred_element_type=f32)
-            + jnp.dot(hi, wl, preferred_element_type=f32)
-        )
-        image_ref[:, pl.ds(at, PIX)] = image[6:9]
+        for u in range(2):
+            two = pixel_sum(jnp.concatenate([t_hi[u], t_mid[u]], axis=0), wh_s[u])
+            got = (
+                pixel_sum(basis, gh_s[u])
+                + pixel_sum(basis, gl_s[u])
+                + two[:16]
+                + two[16:]
+                + pixel_sum(t_hi[u], wl_s[u])
+            )
+            for c in range(4):
+                at_c = pl.multiple_of((8 * p + 4 * u + c) * 16, 16)
+                sums[pl.ds(at_c, 16), :] = got[:, c * LANES : (c + 1) * LANES]
+            two = jnp.dot(jnp.concatenate([hi[u], mid[u]], axis=0), wh_s[u], preferred_element_type=f32)
+            image = two[:16] + two[16:] + jnp.dot(hi[u], wl_s[u], preferred_element_type=f32)
+            image_ref[:, pl.ds(at[u], PIX)] = image[6:9]
         return 0
 
-    lax.fori_loop(0, TILES, one_tile, 0)
+    lax.fori_loop(0, TILES // 2, one_pair, 0)
 
     s = [sums[pl.ds(q, ROWS, stride=16), :] for q in range(PROJ)]
     mx, my, ca, cb, cc = (where_s[r] for r in range(5))
@@ -507,34 +511,18 @@
     for r in range(PROJ):
         table[r] = jnp.where(live, grads[r], 0.0)
 
+
     def hand(r, at, value):
-        grad_ref[at : at + value.shape[0], r, :] = value
-
-    regroup(table, ROWS, group_ref[...], hand)
-
-
-def add_kernel(asked_ref, grad_ref, sum_ref, acc, low_s, *scratch):
-    greet()
-    back = Exchange(grad_ref, *scratch)
-    near, far = scratch[:2]
-    low_id = iota((PIX, PIX), 0)
-    high_id = iota((32, PIX), 0)
-
-    def find(i, _):
-        index = jnp.concatenate([asked_ref[pl.ds(2 * i, 1), :], asked_ref[pl.ds(2 * i + 1, 1), :]], axis=1)
-        at = pl.multiple_of(i * PIX, PIX)
-        low_s[pl.ds(at, PIX), :] = jnp.where(low_id == jnp.bitwise_and(index, 255), 1.0, 0.0).astype(bf16)
-        return 0
-
-    met()
+        grad_box[at : at + value.shape[0], r, :] = value
+
+    regroup(table, ROWS, group_s[...], hand)
     back.send()
-    lax.fori_loop(0, ROWS // 2, find, 0)
-    acc[...] = jnp.zeros_like(acc)
     back.receive()
+
     mine = lax.shift_right_logical(iota((PROJ, LANES), 1), 6) == back.core
 
     def add(i, _):
-        index = jnp.concatenate([asked_ref[pl.ds(2 * i, 1), :], asked_ref[pl.ds(2 * i + 1, 1), :]], axis=1)
+        index = jnp.concatenate([asked_s[pl.ds(2 * i, 1), :], asked_s[pl.ds(2 * i + 1, 1), :]], axis=1)
         here = high_id == lax.shift_right_logical(index, 8)
         halves = []
         for j in range(2):
@@ -598,64 +586,50 @@
     return jax.ShapeDtypeStruct(shape, dtype)
 
 
-def fetch(counts, angles, owners, locals_, gaussians):
-    box = sds((ROWS, LANES), i32)
+def splat(counts, order, angles, owners, locals_, cot, gaussians):
+    square = pltpu.VMEM((ROWS, LANES), i32)
+    pair = pltpu.VMEM((2, SLOTS, PIX), f32)
+    pair_half = pltpu.VMEM((2, SLOTS, PIX), bf16)
+    values = pltpu.VMEM((PROJ, ROWS, LANES), f32)
+    lines = pltpu.VMEM((ROWS * 16, LANES), f32)
     return pl.pallas_call(
-        fetch_kernel,
-        out_shape=(sds((PROJ, ROWS, LANES)), box, box, box),
-        in_specs=[SMEM, SMEM, VMEM, VMEM, ANY],
-        out_specs=(VMEM, VMEM, VMEM, VMEM),
+        splat_kernel,
+        out_shape=(sds(cot.shape), sds((PROJ, ROWS, LANES))),
+        in_specs=[SMEM, SMEM, SMEM, VMEM, VMEM, VMEM, ANY],
+        out_specs=(VMEM, VMEM),
         scratch_shapes=[
             pltpu.VMEM((TILES, SLOTS), i32),
             pltpu.VMEM((TILES, SLOTS), i32),
             pltpu.VMEM((DEVS, 256), f32),
             pltpu.VMEM((256, LANES), f32),
             pltpu.VMEM(gaussians.shape, f32),
-            pltpu.VMEM((ROWS * 16, LANES), f32),
-            pltpu.VMEM((PROJ, ROWS, LANES), f32),
+            lines,
+            values,
+            values,
+            square,
+            square,
+            square,
+            lines,
+            lines,
+            pair,
+            pair,
+            pair,
+            pair_half,
+            pair_half,
+            pair_half,
+            pair_half,
+            pltpu.VMEM((64 * PROJ, PIX), f32),
+            pltpu.VMEM((TILES * SLOTS, PIX), bf16),
             pltpu.SemaphoreType.DMA,
         ]
         + exchange_scratch(1, i32)
+        + exchange_scratch(PROJ, f32)
         + exchange_scratch(PROJ, f32),
-        compiler_params=pltpu.CompilerParams(collective_id=0, has_side_effects=True),
-        name="fetch",
-    )(counts, angles, owners, locals_, gaussians)
-
-
-def render(counts, order, got, pos, group, cot):
-    return pl.pallas_call(
-        render_kernel,
-        out_shape=(sds((3, TILES * PIX)), sds((ROWS, PROJ, LANES))),
-        in_specs=[SMEM, SMEM, VMEM, VMEM, VMEM, VMEM],
-        out_specs=(VMEM, VMEM),
-        scratch_shapes=[
-            pltpu.VMEM((PROJ, ROWS, LANES), f32),
-            pltpu.VMEM((PROJ, ROWS, LANES), f32),
-            pltpu.VMEM((ROWS * 16, LANES), f32),
-            pltpu.VMEM((ROWS * 16, LANES), f32),
-            pltpu.VMEM((SLOTS, PIX), f32),
-            pltpu.VMEM((SLOTS, PIX), f32),
-            pltpu.VMEM((SLOTS, PIX), f32),
-            pltpu.VMEM((SLOTS, PIX), bf16),
-            pltpu.VMEM((SLOTS, PIX), bf16),
-            pltpu.VMEM((SLOTS, PIX), bf16),
-            pltpu.VMEM((SLOTS, PIX), bf16),
-        ],
-        name="render",
-    )(counts, order, got, pos, group, cot)
-
-
-def add(asked, grads):
-    return pl.pallas_call(
-        add_kernel,
-        out_shape=sds((PROJ, ROWS, LANES)),
-        in_specs=[VMEM, VMEM],
-        out_specs=VMEM,
-        scratch_shapes=[pltpu.VMEM((64 * PROJ, PIX), f32), pltpu.VMEM((TILES * SLOTS, PIX), bf16)]
-        + exchange_scratch(PROJ, f32)[1:],
-        compiler_params=pltpu.CompilerParams(collective_id=1, has_side_effects=True),
-        name="add",
-    )(asked, grads)
+        compiler_params=pltpu.CompilerParams(
+            collective_id=0, has_side_effects=True, vmem_limit_bytes=40 * 1024 * 1024
+        ),
+        name="splat",
+    )(counts, order, angles, owners, locals_, cot, gaussians)
 
 
 def pull(angles, gaussians, sums):
@@ -670,9 +644,10 @@
 
 
 def shards(gaussians, view_angles, tile_order, tile_owners, tile_locals, list_counts, image_cotangent):
-    got, asked, pos, group = fetch(list_counts, view_angles, tile_owners, tile_locals, gaussians)
-    rendered, slot_grads = render(list_counts, tile_order, got, pos, group, image_cotangent)
-    return rendered, pull(view_angles, gaussians, add(asked, slot_grads))
+    rendered, sums = splat(
+        list_counts, tile_order, view_angles, tile_owners, tile_locals, image_cotangent, gaussians
+    )
+    return rendered, pull(view_angles, gaussians, sums)
 
 
 def solution(mesh):

time: 111 us -> 96.5 us (0.87)
  Pallas kernels: 110 us -> 88.2 us
  local copies, waits for them, and re-layouts: 0 us -> 7.25 us
    pallas_call x3 -> x1, Pallas kernels: 107 us -> 84.4 us  [splat(): pl.pallas_call(splat_kernel, out_shape=(sds(cot.shape), sds((PROJ, ROWS,...]
    unnamed x0 -> x17, local copies, waits for them, and re-layouts: none -> 7.25 us
where the time goes in v3:
time: 96.5 us; the launch traced here: 96.1 us
  Pallas kernels  88.2 us (91%)
  local copies, waits for them, and re-layouts  7.25 us (8%)
    pallas_call x1, Pallas kernels, splat(): pl.pallas_call(splat_kernel, out_shape=(sds(cot.shape), sds((PROJ, ROWS,...  84.4 us
    unnamed x17, local copies, waits for them, and re-layouts  7.25 us
    pallas_call x1, Pallas kernels, pull(): pl.pallas_call(pull_kernel, out_shape=sds(gaussians.shape), in_specs=[SME...  3.81 us

profile of v3, /device:TPU:1, one launch (start us, length us, event | category | flops | bytes accessed | tf_op | source)
XLA Modules:
  0.0 96.1 jit_solution(10599407101977472822)
XLA Ops:
  0.6 0.0 copy-start
  0.6 1.6 %copy-done = f32[59,8192]{1,0:T(8,128)S(1)} copy-done((f32[59,8192]{1,0:T(8,128)S(1)}, f32[59,8192]{1,0:T(8,128)}, u32[]{:S(2)}) %copy-start) | copy-done | bytes 1933336
  2.2 0.0 copy-start.2
  2.2 0.8 copy-done.2
  3.1 0.0 copy-start.3
  3.1 0.8 copy-done.3
  3.8 0.0 copy-start.4
  3.8 0.8 copy-done.4
  4.6 0.0 copy-start.5
  4.6 0.7 copy-done.5
  5.2 0.0 copy-start.6
  5.2 0.7 copy-done.6
  5.9 0.0 copy-start.7
  5.9 0.7 copy-done.7
  6.5 84.4 %splat.1 = (f32[3,4096]{1,0:T(4,128)S(1)}, f32[9,64,128]{2,1,0:T(8,128)S(1)}) custom-call(s32[16]{0:T(128)S(1)} %copy-done.6, s32[16]{0:T(128)S(1)} %copy-done.7, f32[3]{0:T(128)S(1)} %copy-done.5, s32[16,512]{1,0:T(8,128)S(1)} %copy-done.3, s32[16,512]{1,0:T(8,128)S(1)} %copy-done.4, f32[3,4096]{1,0:T(4,128)S(1)} %copy-done.2, f32[59,8192]{1,0:T(8,128)S(1)} %copy-done), custom_call_target="tpu_custom_call" | custom-call | tf_op jit(solution)/shard_map/splat/pallas_call | solution.py:595
  90.9 0.0 copy-start.1
  90.9 0.7 copy-done.1
  91.7 3.8 %pull.1 = f32[59,8192]{1,0:T(8,128)} custom-call(f32[3]{0:T(128)} %angle_ref.3, f32[59,8192]{1,0:T(8,128)} %gauss_ref.1, f32[9,64,128]{2,1,0:T(8,128)} %copy-done.1), custom_call_target="tpu_custom_call" | custom-call | tf_op jit(solution)/shard_map/pull/pallas_call | solution.py:636
  95.5 0.6 copy.10
Async XLA Ops:
  0.6 1.6 %copy-start = (f32[59,8192]{1,0:T(8,128)S(1)}, f32[59,8192]{1,0:T(8,128)}, u32[]{:S(2)}) copy-start(f32[59,8192]{1,0:T(8,128)} %gauss_ref.1) | copy-start | bytes 5799940
  2.2 0.8 copy-start.2
  3.1 0.8 copy-start.3
  3.8 0.8 copy-start.4
  4.6 0.7 copy-start.5
  5.2 0.7 copy-start.6
  5.9 0.7 copy-start.7
  90.9 0.7 copy-start.1

commit v4 on v3

--- a/solution.py
+++ b/solution.py
@@ -82,6 +82,7 @@
 
 
 COLOUR_ROWS = ((8, 32), (24, 48), (40, 59))
+VIEW_ROWS = 80
 
 
 def colour_weights(basis):
@@ -119,25 +120,46 @@
     return mean_x, mean_y, cov_c * inv, -cov_b * inv, cov_a * inv, log_opacity
 
 
-def regroup(table_ref, rows_of, index, store):
-    part_rows = 16
-    for part in range(ROWS // part_rows):
-        flat = index[part * part_rows : (part + 1) * part_rows]
+def regroup(table_ref, parts_s, index_ref, store, done=None, start=0):
+    for r in range(PROJ):
+        even = table_ref[r, pl.ds(0, 32, stride=2), :]
+        odd = table_ref[r, pl.ds(1, 32, stride=2), :]
+        for n, part in enumerate(split3(jnp.concatenate([even, odd], axis=1))):
+            parts_s[r * 32 : (r + 1) * 32, n * PIX : (n + 1) * PIX] = part
+    high_id = iota((32, PIX), 0)
+    low_id = iota((PIX, PIX), 0)
+
+    def step(n, _):
+        g = (n + start) % 4
+        at = pl.multiple_of(8 * g, 8)
+        flat = index_ref[pl.ds(at, 8), :]
         high = lax.shift_right_logical(flat, 7)
         low = jnp.bitwise_and(flat, 127)
-
-        def step(i, held):
+        held = [jnp.zeros((8, LANES), f32)] * PROJ
+        for i in range(ROWS):
             here = high == i
-            out = []
             for r in range(PROJ):
-                row = jnp.broadcast_to(table_ref[r, pl.ds(i, 1), :], (part_rows, LANES))
-                out.append(jnp.where(here, lane_pick(row, low), held[r]))
-            return tuple(out)
-
-        start = tuple(jnp.zeros((part_rows, LANES), f32) for _ in range(PROJ))
-        taken = lax.fori_loop(0, ROWS, step, start, unroll=16)
+                row = jnp.broadcast_to(table_ref[r, i : i + 1, :], (8, LANES))
+                held[r] = jnp.where(here, lane_pick(row, low), held[r])
         for r in range(PROJ):
-            store(r, part * part_rows, taken[r])
+            store(r, at, held[r])
+        for q in range(4):
+            line = 32 + 8 * g + 2 * q
+            index = jnp.concatenate([index_ref[pl.ds(line, 1), :], index_ref[pl.ds(line + 1, 1), :]], axis=1)
+            column = jnp.where(low_id == jnp.bitwise_and(index, 255), 1.0, 0.0).astype(bf16)
+            here = high_id == lax.shift_right_logical(index, 8)
+            got = jnp.dot(
+                parts_s[...], jnp.concatenate([column] * 3, axis=0), preferred_element_type=f32
+            )
+            for r in range(PROJ):
+                value = jnp.sum(jnp.where(here, got[r * 32 : (r + 1) * 32], 0.0), axis=0, keepdims=True)
+                store(r, line, value[:, :LANES])
+                store(r, line + 1, value[:, LANES:])
+        if done is not None:
+            done(g)
+        return 0
+
+    lax.fori_loop(0, 4, step, 0)
 
 
 def slot_of(row):
@@ -190,7 +212,7 @@
             )
         return 0
 
-    lax.fori_loop(0, TILES, step, 0)
+    lax.fori_loop(0, TILES, step, 0, unroll=4)
     total = sum_s[...].astype(i32)
     want_ref[:, 0, :] = total[0:64] * 128 + total[64:128]
     group_ref[...] = total[128:192] * 128 + total[192:256]
@@ -237,6 +259,22 @@
         lax.fori_loop(1, CHIPS, one, 0)
         self.refs[1][self.chip] = self.refs[0][self.chip]
 
+    def send_group(self, g):
+        def one(n, _):
+            to = 8 * g + n % 8 + 32 * (n // 8)
+            i = (to + CHIPS - self.chip) % CHIPS
+
+            @pl.when(i > 0)
+            def _():
+                self.copy(i).start()
+
+            return 0
+
+        lax.fori_loop(0, 16, one, 0)
+
+    def keep_own(self):
+        self.refs[1][self.chip] = self.refs[0][self.chip]
+
     def receive(self):
         _, near, far = self.refs
 
@@ -293,17 +331,16 @@
     return [box, box, box, sem, sem, pltpu.SemaphoreType.DMA((2,))]
 
 
-def spread(gauss_ref, held, row_of):
-    for i in range(ROWS):
-        at = row_of(i) * 16
-        held[at : at + 16, :] = gauss_ref[0:16, i * LANES : (i + 1) * LANES]
-    return [held[pl.ds(r, ROWS, stride=16), :] for r in range(11)]
+def spread(gauss_ref, held, tiles):
+    for i in range(tiles):
+        held[i * 16 : i * 16 + 16, :] = gauss_ref[0:16, i * LANES : (i + 1) * LANES]
+    return [held[pl.ds(r, tiles, stride=16), :] for r in range(11)]
 
 
 def splat_kernel(
-    count_ref, order_ref, angle_ref, owner_ref, local_ref, cot_ref, gauss_hbm, image_ref, sum_ref,
+    count_ref, order_ref, angle_ref, owner_ref, local_ref, cot_ref, gauss_hbm, image_ref, sum_ref, view_ref,
     own_s, loc_s, carry_s, sum_s, gauss_ref, held, table, where_s, pos_s, group_s, asked_s, coef, sums,
-    alpha_s, w_s, v_s, gh_s, gl_s, wh_s, wl_s, acc, low_s, load_sem, *boxes,
+    alpha_s, w_s, v_s, gh_s, gl_s, wh_s, wl_s, acc, low_s, parts_s, load_sem, *boxes,
 ):
     load = pltpu.make_async_copy(gauss_hbm, gauss_ref, load_sem)
     load.start()
@@ -318,8 +355,12 @@
 
     first, second, third = view_of(angle_ref)
     weights = colour_weights(harmonics(*third))
+    for n, entry in enumerate(first + second):
+        view_ref[n : n + 1, :] = entry
+    for c, (low, high) in enumerate(COLOUR_ROWS):
+        view_ref[8 + 24 * c : 8 + 24 * c + high - low, :] = weights[c]
     load.wait()
-    params = spread(gauss_ref, held, lambda i: i)
+    params = spread(gauss_ref, held, ROWS)
     for r, value in enumerate(project(params, first, second)):
         table[r] = value
     for i in range(ROWS):
@@ -333,10 +374,11 @@
     asked_s[...] = ask.row(0)
 
     def answer(r, at, value):
-        picked[at : at + value.shape[0], r, :] = value
-
-    regroup(table, ROWS, asked_s[...], answer)
-    reply.send()
+        picked[pl.ds(at, value.shape[0]), r, :] = value
+
+    turn = ask.chip // 8
+    regroup(table, parts_s, asked_s, answer, reply.send_group, turn)
+    reply.keep_own()
 
     low_id = iota((PIX, PIX), 0)
     high_id = iota((32, PIX), 0)
@@ -366,9 +408,9 @@
         table[r] = reply.row(r)
 
     def keep(r, at, value):
-        where_s[r, at : at + value.shape[0], :] = value
-
-    regroup(table, ROWS, pos_s[...], keep)
+        where_s[r, pl.ds(at, value.shape[0]), :] = value
+
+    regroup(table, parts_s, pos_s, keep)
     mx = where_s[0] - mid_x
     my = where_s[1] - mid_y
     ca, cb, cc = where_s[2], where_s[3], where_s[4]
@@ -513,10 +555,10 @@
 
 
     def hand(r, at, value):
-        grad_box[at : at + value.shape[0], r, :] = value
-
-    regroup(table, ROWS, group_s[...], hand)
-    back.send()
+        grad_box[pl.ds(at, value.shape[0]), r, :] = value
+
+    regroup(table, parts_s, group_s, hand, back.send_group, turn)
+    back.keep_own()
     back.receive()
 
     mine = lax.shift_right_logical(iota((PROJ, LANES), 1), 6) == back.core
@@ -543,32 +585,29 @@
         )
         return 0
 
-    lax.fori_loop(0, ROWS // 2, add, 0)
+    lax.fori_loop(0, ROWS // 2, add, 0, unroll=4)
     for r in range(PROJ):
         both = acc[64 * r : 64 * r + 32, :] + acc[64 * r + 32 : 64 * r + 64, :]
-        sum_ref[r] = jnp.concatenate([both[:, :LANES], both[:, LANES:]], axis=0)
-
-
-def pull_kernel(angle_ref, gauss_ref, sum_ref, out_ref, held):
-    first, second, third = view_of(angle_ref)
-    weights = colour_weights(harmonics(*third))
-
-    def row_of(i):
-        return (i % 2) * 32 + i // 2
-
-    params = spread(gauss_ref, held, row_of)
+        sum_ref[r, pl.ds(0, 32, stride=2), :] = both[:, :LANES]
+        sum_ref[r, pl.ds(1, 32, stride=2), :] = both[:, LANES:]
+
+
+def pull_kernel(view_ref, gauss_ref, sum_ref, out_ref, held):
+    tiles = sum_ref.shape[1]
+    first = tuple(view_ref[n : n + 1, :] for n in range(3))
+    second = tuple(view_ref[n : n + 1, :] for n in range(3, 6))
+    w0, w1, w2 = (view_ref[8 + 24 * c : 8 + 24 * c + high - low, :] for c, (low, high) in enumerate(COLOUR_ROWS))
+    params = spread(gauss_ref, held, tiles)
     _, pullback = jax.vjp(lambda *p: project(p, first, second), *params)
     grads = pullback(tuple(sum_ref[r] for r in range(6)))
     held[...] = jnp.zeros_like(held)
     for r in range(11):
-        held[pl.ds(r, ROWS, stride=16), :] = grads[r]
-    w0, w1, w2 = weights
-    for i in range(ROWS):
-        at = row_of(i)
+        held[pl.ds(r, tiles, stride=16), :] = grads[r]
+    for i in range(tiles):
         lanes = slice(i * LANES, (i + 1) * LANES)
-        tint = [sum_ref[6 + c, at : at + 1, :] for c in range(3)]
-        out_ref[0:8, lanes] = held[at * 16 : at * 16 + 8, :]
-        out_ref[8:16, lanes] = held[at * 16 + 8 : at * 16 + 16, :] + w0[0:8] * tint[0]
+        tint = [sum_ref[6 + c, i : i + 1, :] for c in range(3)]
+        out_ref[0:8, lanes] = held[i * 16 : i * 16 + 8, :]
+        out_ref[8:16, lanes] = held[i * 16 + 8 : i * 16 + 16, :] + w0[0:8] * tint[0]
         out_ref[16:24, lanes] = w0[8:16] * tint[0]
         out_ref[24:32, lanes] = w0[16:24] * tint[0] + w1[0:8] * tint[1]
         out_ref[32:40, lanes] = w1[8:16] * tint[1]
@@ -594,9 +633,9 @@
     lines = pltpu.VMEM((ROWS * 16, LANES), f32)
     return pl.pallas_call(
         splat_kernel,
-        out_shape=(sds(cot.shape), sds((PROJ, ROWS, LANES))),
+        out_shape=(sds(cot.shape), sds((PROJ, ROWS, LANES)), sds((VIEW_ROWS, LANES))),
         in_specs=[SMEM, SMEM, SMEM, VMEM, VMEM, VMEM, ANY],
-        out_specs=(VMEM, VMEM),
+        out_specs=(VMEM, VMEM, VMEM),
         scratch_shapes=[
             pltpu.VMEM((TILES, SLOTS), i32),
             pltpu.VMEM((TILES, SLOTS), i32),
@@ -620,34 +659,42 @@
             pair_half,
             pltpu.VMEM((64 * PROJ, PIX), f32),
             pltpu.VMEM((TILES * SLOTS, PIX), bf16),
+            pltpu.VMEM((32 * PROJ, 3 * PIX), bf16),
             pltpu.SemaphoreType.DMA,
         ]
         + exchange_scratch(1, i32)
         + exchange_scratch(PROJ, f32)
         + exchange_scratch(PROJ, f32),
         compiler_params=pltpu.CompilerParams(
-            collective_id=0, has_side_effects=True, vmem_limit_bytes=40 * 1024 * 1024
+            collective_id=0, has_side_effects=True, vmem_limit_bytes=60 * 1024 * 1024
         ),
         name="splat",
     )(counts, order, angles, owners, locals_, cot, gaussians)
 
 
-def pull(angles, gaussians, sums):
+def pull(view, gaussians, sums, steps=4):
+    tiles = ROWS // steps
+    slab = pl.BlockSpec((gaussians.shape[0], tiles * LANES), lambda i: (0, i))
     return pl.pallas_call(
         pull_kernel,
+        grid=(steps,),
         out_shape=sds(gaussians.shape),
-        in_specs=[SMEM, VMEM, VMEM],
-        out_specs=VMEM,
-        scratch_shapes=[pltpu.VMEM((ROWS * 16, LANES), f32)],
+        in_specs=[
+            pl.BlockSpec((VIEW_ROWS, LANES), lambda i: (0, 0)),
+            slab,
+            pl.BlockSpec((PROJ, tiles, LANES), lambda i: (0, i, 0)),
+        ],
+        out_specs=slab,
+        scratch_shapes=[pltpu.VMEM((tiles * 16, LANES), f32)],
         name="pull",
-    )(angles, gaussians, sums)
+    )(view, gaussians, sums)
 
 
 def shards(gaussians, view_angles, tile_order, tile_owners, tile_locals, list_counts, image_cotangent):
-    rendered, sums = splat(
+    rendered, sums, view = splat(
         list_counts, tile_order, view_angles, tile_owners, tile_locals, image_cotangent, gaussians
     )
-    return rendered, pull(view_angles, gaussians, sums)
+    return rendered, pull(view, gaussians, sums)
 
 
 def solution(mesh):

time: 96.5 us -> 72.4 us (0.75)
  Pallas kernels: 88.2 us -> 70.9 us
  local copies, waits for them, and re-layouts: 7.25 us -> 0.63 us
    pallas_call x1, Pallas kernels: 84.4 us -> 66.7 us  [splat(): pl.pallas_call(splat_kernel, out_shape=(sds(cot.shape), sds((PROJ, ROWS,...]
    unnamed x17 -> x3, local copies, waits for them, and re-layouts: 7.25 us -> 0.63 us
where the time goes in v4:
time: 72.4 us; the launch traced here: 72.2 us
  Pallas kernels  70.9 us (98%)
    pallas_call x1, Pallas kernels, splat(): pl.pallas_call(splat_kernel, out_shape=(sds(cot.shape), sds((PROJ, ROWS,...  66.7 us
    pallas_call x1, Pallas kernels, pull(): pl.pallas_call(pull_kernel, grid=(steps,), out_shape=sds(gaussians.shape)...  4.13 us

profile of v4, /device:TPU:1, one launch (start us, length us, event | category | flops | bytes accessed | tf_op | source)
XLA Modules:
  0.0 72.2 jit_solution(10608041710853075016)
XLA Ops:
  0.6 66.7 %splat.1 = (f32[3,4096]{1,0:T(4,128)}, f32[9,64,128]{2,1,0:T(8,128)}, f32[80,128]{1,0:T(8,128)}) custom-call(s32[16]{0:T(128)} %count_ref.1, s32[16]{0:T(128)} %order_ref.1, f32[3]{0:T(128)} %angle_ref.1, s32[16,512]{1,0:T(8,128)} %owner_ref.1, s32[16,512]{1,0:T(8,128)} %local_ref.1, f32[3,4096]{1,0:T(4,128)} %cot_ref.1, f32[59,8192]{1,0:T(8,128)} %gauss_ref.1), custom_call_target="tpu_custom_call" | custom-call | tf_op jit(solution)/shard_map/splat/pallas_call | solution.py:634
  67.4 0.0 copy-start
  67.4 4.1 %pull.1 = f32[59,8192]{1,0:T(8,128)} custom-call(f32[80,128]{1,0:T(8,128)} %get-tuple-element.6.view_ref, f32[59,8192]{1,0:T(8,128)} %gauss_ref.1, f32[9,64,128]{2,1,0:T(8,128)} %get-tuple-element.7.sum_ref), custom_call_target="tpu_custom_call" | custom-call | tf_op jit(solution)/shard_map/pull/pallas_call | solution.py:678
  71.5 0.0 copy-done
  71.5 0.6 copy.10
Async XLA Ops:
  67.4 4.1 %copy-start = (f32[3,4096]{1,0:T(4,128)S(1)}, f32[3,4096]{1,0:T(4,128)}, u32[]{:S(2)}) copy-start(f32[3,4096]{1,0:T(4,128)} %get-tuple-element.10) | copy-start | bytes 147460

commit v5 on v4

--- a/solution.py
+++ b/solution.py
@@ -120,7 +120,11 @@
     return mean_x, mean_y, cov_c * inv, -cov_b * inv, cov_a * inv, log_opacity
 
 
-def regroup(table_ref, parts_s, index_ref, store, done=None, start=0):
+def plane(y, n):
+    return (y + 2 + 3 * n + 3 * (n // 2) + 2 * (n // 3)) % 4
+
+
+def regroup(table_ref, parts_s, index_ref, store, done=None, y=0):
     for r in range(PROJ):
         even = table_ref[r, pl.ds(0, 32, stride=2), :]
         odd = table_ref[r, pl.ds(1, 32, stride=2), :]
@@ -130,8 +134,8 @@
     low_id = iota((PIX, PIX), 0)
 
     def step(n, _):
-        g = (n + start) % 4
-        at = pl.multiple_of(8 * g, 8)
+        g = plane(y, n)
+        at = pl.multiple_of(16 * g, 8)
         flat = index_ref[pl.ds(at, 8), :]
         high = lax.shift_right_logical(flat, 7)
         low = jnp.bitwise_and(flat, 127)
@@ -144,7 +148,7 @@
         for r in range(PROJ):
             store(r, at, held[r])
         for q in range(4):
-            line = 32 + 8 * g + 2 * q
+            line = 16 * g + 8 + 2 * q
             index = jnp.concatenate([index_ref[pl.ds(line, 1), :], index_ref[pl.ds(line + 1, 1), :]], axis=1)
             column = jnp.where(low_id == jnp.bitwise_and(index, 255), 1.0, 0.0).astype(bf16)
             here = high_id == lax.shift_right_logical(index, 8)
@@ -225,85 +229,84 @@
         me = lax.axis_index("dev")
         self.chip = me // 2
         self.core = me % 2
+        self.y = self.chip // 16
         self.other = self.chip * 2 + (1 - self.core)
 
-    def copy(self, i):
+    def copy(self, to):
         x_ref, near, _ = self.refs
-        to = (self.chip + i) % CHIPS
         return pltpu.make_async_remote_copy(
             src_ref=x_ref.at[to],
             dst_ref=near.at[self.chip],
-            send_sem=self.sems[0].at[i],
-            recv_sem=self.sems[1].at[i],
+            send_sem=self.sems[0].at[0],
+            recv_sem=self.sems[1].at[self.y],
             device_id=(to * 2 + self.core,),
             device_id_type=MESH,
         )
 
-    def incoming(self, i):
+    def many(self, row, count, g):
         x_ref, near, _ = self.refs
-        source = (self.chip + CHIPS - i) % CHIPS
         return pltpu.make_async_remote_copy(
-            src_ref=x_ref.at[source],
-            dst_ref=near.at[source],
-            send_sem=self.sems[0].at[i],
-            recv_sem=self.sems[1].at[i],
-            device_id=(source * 2 + self.core,),
-            device_id_type=MESH,
-        )
-
-    def send(self):
-        def one(i, _):
-            self.copy(i).start()
-            return 0
-
-        lax.fori_loop(1, CHIPS, one, 0)
-        self.refs[1][self.chip] = self.refs[0][self.chip]
-
-    def send_group(self, g):
-        def one(n, _):
-            to = 8 * g + n % 8 + 32 * (n // 8)
-            i = (to + CHIPS - self.chip) % CHIPS
-
-            @pl.when(i > 0)
-            def _():
-                self.copy(i).start()
-
-            return 0
-
-        lax.fori_loop(0, 16, one, 0)
-
-    def keep_own(self):
-        self.refs[1][self.chip] = self.refs[0][self.chip]
-
-    def receive(self):
-        _, near, far = self.refs
-
-        def arrived(i, _):
-            self.incoming(i).wait_recv()
-            return 0
-
-        lax.fori_loop(1, CHIPS, arrived, 0)
-        swap = pltpu.make_async_remote_copy(
-            src_ref=near,
-            dst_ref=far,
-            send_sem=self.sems[2].at[0],
-            recv_sem=self.sems[2].at[1],
+            src_ref=x_ref.at[pl.ds(row, count)],
+            dst_ref=near.at[pl.ds(row, count)],
+            send_sem=self.sems[0].at[0],
+            recv_sem=self.sems[1].at[g],
             device_id=(self.other,),
             device_id_type=MESH,
         )
-        swap.start()
-
-        def sent(i, _):
-            self.copy(i).wait_send()
+
+    def send_group(self, g):
+        def one(n, _):
+            to = 16 * g + (self.chip + n) % 16
+
+            @pl.when(to != self.chip)
+            def _():
+                self.copy(to).start()
+
             return 0
 
-        lax.fori_loop(1, CHIPS, sent, 0)
-        swap.wait()
-
-    def row(self, r):
+        lax.fori_loop(0, 16, one, 0, unroll=4)
+
+    def keep_own(self):
+        self.refs[1][self.chip] = self.refs[0][self.chip]
+
+    def send(self):
+        for n in range(4):
+            self.send_group(plane(self.y, n))
+        self.keep_own()
+
+    def wait_group(self, n):
+        g = plane(self.y, n)
+        self.many(16 * g, 16 if n < 3 else 15, g).wait_recv()
+
+    def swap(self, n):
         _, near, far = self.refs
-        mine = lax.shift_right_logical(iota((CHIPS, LANES), 1), 6) == self.core
-        return jnp.where(mine, near[:, r, :], pltpu.roll(far[:, r, :], 64, 1))
+        rows = pl.ds(16 * plane(self.y, n), 16)
+        return pltpu.make_async_remote_copy(
+            src_ref=near.at[rows],
+            dst_ref=far.at[rows],
+            send_sem=self.sems[2].at[n],
+            recv_sem=self.sems[2].at[4 + n],
+            device_id=(self.other,),
+            device_id_type=MESH,
+        )
+
+    def receive(self, work):
+        for n in range(4):
+            self.wait_group(n)
+            self.swap(n).start()
+            if n > 0:
+                self.swap(n - 1).wait()
+                work(plane(self.y, n - 1))
+
+        self.many(0, CHIPS - 1, 0).wait_send()
+        self.swap(3).wait()
+        work(plane(self.y, 3))
+
+    def rows(self, g, r):
+        _, near, far = self.refs
+        at = pl.ds(16 * g, 16)
+        mine = lax.shift_right_logical(iota((16, LANES), 1), 6) == self.core
+        return jnp.where(mine, near[at, r, :], pltpu.roll(far[at, r, :], 64, 1))
 
 
 def greet():
@@ -327,8 +330,8 @@
 
 def exchange_scratch(rows, dtype):
     box = pltpu.VMEM((CHIPS, rows, LANES), dtype)
-    sem = pltpu.SemaphoreType.DMA((CHIPS,))
-    return [box, box, box, sem, sem, pltpu.SemaphoreType.DMA((2,))]
+    sem = pltpu.SemaphoreType.DMA
+    return [box, box, box, sem((1,)), sem((4,)), sem((8,))]
 
 
 def spread(gauss_ref, held, tiles):
@@ -370,14 +373,15 @@
                 gauss_ref[low:high, lanes] * weights[c], axis=0, keepdims=True
             )
 
-    ask.receive()
-    asked_s[...] = ask.row(0)
+    def note(g):
+        asked_s[pl.ds(pl.multiple_of(16 * g, 16), 16), :] = ask.rows(g, 0)
+
+    ask.receive(note)
 
     def answer(r, at, value):
         picked[pl.ds(at, value.shape[0]), r, :] = value
 
-    turn = ask.chip // 8
-    regroup(table, parts_s, asked_s, answer, reply.send_group, turn)
+    regroup(table, parts_s, asked_s, answer, reply.send_group, reply.y)
     reply.keep_own()
 
     low_id = iota((PIX, PIX), 0)
@@ -403,9 +407,12 @@
     live = slot < count
     mid_x = (jnp.bitwise_and(shown, TX - 1) * 16 + 8).astype(f32)
     mid_y = (lax.shift_right_logical(shown, 5) * 16 + 8).astype(f32)
-    reply.receive()
-    for r in range(PROJ):
-        table[r] = reply.row(r)
+
+    def collect(g):
+        for r in range(PROJ):
+            table[r, pl.ds(pl.multiple_of(16 * g, 16), 16), :] = reply.rows(g, r)
+
+    reply.receive(collect)
 
     def keep(r, at, value):
         where_s[r, pl.ds(at, value.shape[0]), :] = value
@@ -557,9 +564,8 @@
     def hand(r, at, value):
         grad_box[pl.ds(at, value.shape[0]), r, :] = value
 
-    regroup(table, parts_s, group_s, hand, back.send_group, turn)
+    regroup(table, parts_s, group_s, hand, back.send_group, back.y)
     back.keep_own()
-    back.receive()
 
     mine = lax.shift_right_logical(iota((PROJ, LANES), 1), 6) == back.core
 
@@ -585,7 +591,10 @@
         )
         return 0
 
-    lax.fori_loop(0, ROWS // 2, add, 0, unroll=4)
+    def add_plane(g):
+        lax.fori_loop(0, 8, lambda n, _: add(8 * g + n, 0), 0, unroll=4)
+
+    back.receive(add_plane)
     for r in range(PROJ):
         both = acc[64 * r : 64 * r + 32, :] + acc[64 * r + 32 : 64 * r + 64, :]
         sum_ref[r, pl.ds(0, 32, stride=2), :] = both[:, :LANES]
@@ -672,7 +681,7 @@
     )(counts, order, angles, owners, locals_, cot, gaussians)
 
 
-def pull(view, gaussians, sums, steps=4):
+def pull(view, gaussians, sums, steps=2):
     tiles = ROWS // steps
     slab = pl.BlockSpec((gaussians.shape[0], tiles * LANES), lambda i: (0, i))
     return pl.pallas_call(

time: 72.4 us -> 64.5 us (0.89)
  Pallas kernels: 70.9 us -> 63 us
    pallas_call x1, Pallas kernels: 66.7 us -> 60 us  [splat(): pl.pallas_call(splat_kernel, out_shape=(sds(cot.shape), sds((PROJ, ROWS,...]
    pallas_call x1, Pallas kernels: 4.13 us -> 3.02 us  [pull(): pl.pallas_call(pull_kernel, grid=(steps,), out_shape=sds(gaussians.shape)...]
where the time goes in v5:
time: 64.5 us; the launch traced here: 64.3 us
  Pallas kernels  63 us (98%)
  between operations  0.65 us (1%)
    pallas_call x1, Pallas kernels, splat(): pl.pallas_call(splat_kernel, out_shape=(sds(cot.shape), sds((PROJ, ROWS,...  60 us
    pallas_call x1, Pallas kernels, pull(): pl.pallas_call(pull_kernel, grid=(steps,), out_shape=sds(gaussians.shape)...  3.02 us

profile of v5, /device:TPU:1, one launch (start us, length us, event | category | flops | bytes accessed | tf_op | source)
XLA Modules:
  0.0 64.3 jit_solution(3117364418960425112)
XLA Ops:
  0.6 60.0 %splat.1 = (f32[3,4096]{1,0:T(4,128)}, f32[9,64,128]{2,1,0:T(8,128)}, f32[80,128]{1,0:T(8,128)}) custom-call(s32[16]{0:T(128)} %count_ref.1, s32[16]{0:T(128)} %order_ref.1, f32[3]{0:T(128)} %angle_ref.1, s32[16,512]{1,0:T(8,128)} %owner_ref.1, s32[16,512]{1,0:T(8,128)} %local_ref.1, f32[3,4096]{1,0:T(4,128)} %cot_ref.1, f32[59,8192]{1,0:T(8,128)} %gauss_ref.1), custom_call_target="tpu_custom_call" | custom-call | tf_op jit(solution)/shard_map/splat/pallas_call | solution.py:643
  60.6 0.0 copy-start
  60.6 3.0 %pull.1 = f32[59,8192]{1,0:T(8,128)} custom-call(f32[80,128]{1,0:T(8,128)} %get-tuple-element.6.view_ref, f32[59,8192]{1,0:T(8,128)} %gauss_ref.1, f32[9,64,128]{2,1,0:T(8,128)} %get-tuple-element.7.sum_ref), custom_call_target="tpu_custom_call" | custom-call | tf_op jit(solution)/shard_map/pull/pallas_call | solution.py:687
  63.7 0.0 copy-done
  63.7 0.6 copy.10
Async XLA Ops:
  60.6 3.0 %copy-start = (f32[3,4096]{1,0:T(4,128)S(1)}, f32[3,4096]{1,0:T(4,128)}, u32[]{:S(2)}) copy-start(f32[3,4096]{1,0:T(4,128)} %get-tuple-element.10) | copy-start | bytes 147460

commit v6 on v5

--- a/solution.py
+++ b/solution.py
@@ -341,17 +341,25 @@
 
 
 def splat_kernel(
-    count_ref, order_ref, angle_ref, owner_ref, local_ref, cot_ref, gauss_hbm, image_ref, sum_ref, view_ref,
+    count_ref, order_ref, angle_ref, owner_hbm, local_hbm, cot_hbm, gauss_hbm, image_ref, sum_ref, view_ref,
     own_s, loc_s, carry_s, sum_s, gauss_ref, held, table, where_s, pos_s, group_s, asked_s, coef, sums,
-    alpha_s, w_s, v_s, gh_s, gl_s, wh_s, wl_s, acc, low_s, parts_s, load_sem, *boxes,
+    alpha_s, w_s, v_s, gh_s, gl_s, wh_s, wl_s, acc, low_s, parts_s, owner_ref, local_ref, cot_ref, load_sem, *boxes,
 ):
-    load = pltpu.make_async_copy(gauss_hbm, gauss_ref, load_sem)
-    load.start()
+    loads = [
+        pltpu.make_async_copy(src, dst, load_sem.at[n])
+        for n, (src, dst) in enumerate(
+            ((owner_hbm, owner_ref), (local_hbm, local_ref), (gauss_hbm, gauss_ref), (cot_hbm, cot_ref))
+        )
+    ]
+    for load in loads:
+        load.start()
     greet()
     ask, reply, back = (Exchange(*boxes[6 * n : 6 * n + 6]) for n in range(3))
     wanted, picked, grad_box = boxes[0], boxes[6], boxes[12]
     near, far = boxes[13], boxes[14]
 
+    loads[0].wait()
+    loads[1].wait()
     route(owner_ref, local_ref, wanted, pos_s, group_s, own_s, loc_s, carry_s, sum_s)
     met()
     ask.send()
@@ -362,7 +370,8 @@
         view_ref[n : n + 1, :] = entry
     for c, (low, high) in enumerate(COLOUR_ROWS):
         view_ref[8 + 24 * c : 8 + 24 * c + high - low, :] = weights[c]
-    load.wait()
+    loads[2].wait()
+    loads[3].wait()
     params = spread(gauss_ref, held, ROWS)
     for r, value in enumerate(project(params, first, second)):
         table[r] = value
@@ -601,7 +610,8 @@
         sum_ref[r, pl.ds(1, 32, stride=2), :] = both[:, LANES:]
 
 
-def pull_kernel(view_ref, gauss_ref, sum_ref, out_ref, held):
+def pull_kernel(view_ref, gauss_ref, sum_ref, shot_ref, out_ref, image_ref, held):
+    image_ref[...] = shot_ref[...]
     tiles = sum_ref.shape[1]
     first = tuple(view_ref[n : n + 1, :] for n in range(3))
     second = tuple(view_ref[n : n + 1, :] for n in range(3, 6))
@@ -643,7 +653,7 @@
     return pl.pallas_call(
         splat_kernel,
         out_shape=(sds(cot.shape), sds((PROJ, ROWS, LANES)), sds((VIEW_ROWS, LANES))),
-        in_specs=[SMEM, SMEM, SMEM, VMEM, VMEM, VMEM, ANY],
+        in_specs=[SMEM, SMEM, SMEM, ANY, ANY, ANY, ANY],
         out_specs=(VMEM, VMEM, VMEM),
         scratch_shapes=[
             pltpu.VMEM((TILES, SLOTS), i32),
@@ -669,7 +679,10 @@
             pltpu.VMEM((64 * PROJ, PIX), f32),
             pltpu.VMEM((TILES * SLOTS, PIX), bf16),
             pltpu.VMEM((32 * PROJ, 3 * PIX), bf16),
-            pltpu.SemaphoreType.DMA,
+            pltpu.VMEM(owners.shape, i32),
+            pltpu.VMEM(locals_.shape, i32),
+            pltpu.VMEM(cot.shape, f32),
+            pltpu.SemaphoreType.DMA((4,)),
         ]
         + exchange_scratch(1, i32)
         + exchange_scratch(PROJ, f32)
@@ -681,29 +694,32 @@
     )(counts, order, angles, owners, locals_, cot, gaussians)
 
 
-def pull(view, gaussians, sums, steps=2):
+def pull(view, gaussians, sums, image, steps=2):
     tiles = ROWS // steps
+    shot = pl.BlockSpec((3, image.shape[1] // steps), lambda i: (0, i))
     slab = pl.BlockSpec((gaussians.shape[0], tiles * LANES), lambda i: (0, i))
     return pl.pallas_call(
         pull_kernel,
         grid=(steps,),
-        out_shape=sds(gaussians.shape),
+        out_shape=(sds(gaussians.shape), sds(image.shape)),
         in_specs=[
             pl.BlockSpec((VIEW_ROWS, LANES), lambda i: (0, 0)),
             slab,
             pl.BlockSpec((PROJ, tiles, LANES), lambda i: (0, i, 0)),
+            shot,
         ],
-        out_specs=slab,
+        out_specs=(slab, shot),
         scratch_shapes=[pltpu.VMEM((tiles * 16, LANES), f32)],
         name="pull",
-    )(view, gaussians, sums)
+    )(view, gaussians, sums, image)
 
 
 def shards(gaussians, view_angles, tile_order, tile_owners, tile_locals, list_counts, image_cotangent):
     rendered, sums, view = splat(
         list_counts, tile_order, view_angles, tile_owners, tile_locals, image_cotangent, gaussians
     )
-    return rendered, pull(view, gaussians, sums)
+    gradients, rendered = pull(view, gaussians, sums, rendered)
+    return rendered, gradients
 
 
 def solution(mesh):

time: 64.5 us -> 63.7 us (0.988)
  no operation moved by 1% of the time
where the time goes in v6:
time: 63.7 us; the launch traced here: 63.5 us
  Pallas kernels  62.9 us (99%)
  between operations  0.64 us (1%)
    pallas_call x1, Pallas kernels, splat(): pl.pallas_call(splat_kernel, out_shape=(sds(cot.shape), sds((PROJ, ROWS,...  59.9 us
    pallas_call x1, Pallas kernels, pull(): pl.pallas_call(pull_kernel, grid=(steps,), out_shape=(sds(gaussians.shape...  3.01 us

profile of v6, /device:TPU:1, one launch (start us, length us, event | category | flops | bytes accessed | tf_op | source)
XLA Modules:
  0.0 63.5 jit_solution(9959332505616814844)
XLA Ops:
  0.6 59.9 %splat.1 = (f32[3,4096]{1,0:T(4,128)}, f32[9,64,128]{2,1,0:T(8,128)}, f32[80,128]{1,0:T(8,128)}) custom-call(s32[16]{0:T(128)} %count_ref.1, s32[16]{0:T(128)} %order_ref.1, f32[3]{0:T(128)} %angle_ref.1, s32[16,512]{1,0:T(8,128)} %owner_hbm.1, s32[16,512]{1,0:T(8,128)} %local_hbm.1, f32[3,4096]{1,0:T(4,128)} %cot_hbm.1, f32[59,8192]{1,0:T(8,128)} %gauss_ref.1), custom_call_target="tpu_custom_call" | custom-call | tf_op jit(solution)/shard_map/splat/pallas_call | solution.py:653
  60.5 3.0 %pull.1 = (f32[59,8192]{1,0:T(8,128)}, f32[3,4096]{1,0:T(4,128)}) custom-call(f32[80,128]{1,0:T(8,128)} %get-tuple-element.7.view_ref, f32[59,8192]{1,0:T(8,128)} %gauss_ref.1, f32[9,64,128]{2,1,0:T(8,128)} %get-tuple-element.8.sum_ref, f32[3,4096]{1,0:T(4,128)} %get-tuple-element.9.shot_ref), custom_call_target="tpu_custom_call" | custom-call | tf_op jit(solution)/shard_map/pull/pallas_call | solution.py:701

commit v7 on v6

--- a/solution.py
+++ b/solution.py
@@ -115,7 +115,8 @@
     cov_a = va[0] * va[0] + va[1] * va[1] + va[2] * va[2] + 0.3
     cov_b = va[0] * vb[0] + va[1] * vb[1] + va[2] * vb[2]
     cov_c = vb[0] * vb[0] + vb[1] * vb[1] + vb[2] * vb[2] + 0.3
-    inv = 1.0 / (cov_a * cov_c - cov_b * cov_b)
+    det = cov_a * cov_c - cov_b * cov_b
+    inv = 1.0 / jnp.where(det == 0.0, 1.0, det)
     log_opacity = -jnp.log(1.0 + jnp.exp(-logit))
     return mean_x, mean_y, cov_c * inv, -cov_b * inv, cov_a * inv, log_opacity
 

time: 63.7 us -> 63.7 us (level)
  no operation moved by 1% of the time
where the time goes in v7:
time: 63.7 us; the launch traced here: 63.5 us
  Pallas kernels  62.9 us (99%)
  between operations  0.64 us (1%)
    pallas_call x1, Pallas kernels, splat(): pl.pallas_call(splat_kernel, out_shape=(sds(cot.shape), sds((PROJ, ROWS,...  59.9 us
    pallas_call x1, Pallas kernels, pull(): pl.pallas_call(pull_kernel, grid=(steps,), out_shape=(sds(gaussians.shape...  3.02 us

profile of v7, /device:TPU:1, one launch (start us, length us, event | category | flops | bytes accessed | tf_op | source)
XLA Modules:
  0.0 63.5 jit_solution(5961844470877352232)
XLA Ops:
  0.6 59.9 %splat.1 = (f32[3,4096]{1,0:T(4,128)}, f32[9,64,128]{2,1,0:T(8,128)}, f32[80,128]{1,0:T(8,128)}) custom-call(s32[16]{0:T(128)} %count_ref.1, s32[16]{0:T(128)} %order_ref.1, f32[3]{0:T(128)} %angle_ref.1, s32[16,512]{1,0:T(8,128)} %owner_hbm.1, s32[16,512]{1,0:T(8,128)} %local_hbm.1, f32[3,4096]{1,0:T(4,128)} %cot_hbm.1, f32[59,8192]{1,0:T(8,128)} %gauss_ref.1), custom_call_target="tpu_custom_call" | custom-call | tf_op jit(solution)/shard_map/splat/pallas_call | solution.py:654
  60.5 3.0 %pull.1 = (f32[59,8192]{1,0:T(8,128)}, f32[3,4096]{1,0:T(4,128)}) custom-call(f32[80,128]{1,0:T(8,128)} %get-tuple-element.7.view_ref, f32[59,8192]{1,0:T(8,128)} %gauss_ref.1, f32[9,64,128]{2,1,0:T(8,128)} %get-tuple-element.8.sum_ref, f32[3,4096]{1,0:T(4,128)} %get-tuple-element.9.shot_ref), custom_call_target="tpu_custom_call" | custom-call | tf_op jit(solution)/shard_map/pull/pallas_call | solution.py:702

commit v8 on v7

--- a/solution.py
+++ b/solution.py
@@ -321,7 +321,7 @@
         pl.semaphore_signal(barrier, inc=1, device_id=(peer,), device_id_type=MESH)
         return 0
 
-    lax.fori_loop(1, CHIPS, one, 0)
+    lax.fori_loop(1, CHIPS, one, 0, unroll=9)
     pl.semaphore_signal(barrier, inc=1, device_id=(chip * 2 + (1 - core),), device_id_type=MESH)
 
 
@@ -352,9 +352,9 @@
             ((owner_hbm, owner_ref), (local_hbm, local_ref), (gauss_hbm, gauss_ref), (cot_hbm, cot_ref))
         )
     ]
+    greet()
     for load in loads:
         load.start()
-    greet()
     ask, reply, back = (Exchange(*boxes[6 * n : 6 * n + 6]) for n in range(3))
     wanted, picked, grad_box = boxes[0], boxes[6], boxes[12]
     near, far = boxes[13], boxes[14]
@@ -403,7 +403,7 @@
         low_s[pl.ds(at, PIX), :] = jnp.where(low_id == jnp.bitwise_and(index, 255), 1.0, 0.0).astype(bf16)
         return 0
 
-    lax.fori_loop(0, ROWS // 2, find, 0)
+    lax.fori_loop(0, ROWS // 2, find, 0, unroll=4)
     acc[...] = jnp.zeros_like(acc)
     shape = (ROWS, LANES)
     tile = lax.shift_right_logical(iota(shape, 0), 2)

time: 63.7 us -> 64.1 us (level)
  no operation moved by 1% of the time
where the time goes in v8:
time: 64.1 us; the launch traced here: 63.9 us
  Pallas kernels  63.3 us (99%)
    pallas_call x1, Pallas kernels, splat(): pl.pallas_call(splat_kernel, out_shape=(sds(cot.shape), sds((PROJ, ROWS,...  60.2 us
    pallas_call x1, Pallas kernels, pull(): pl.pallas_call(pull_kernel, grid=(steps,), out_shape=(sds(gaussians.shape...  3.02 us

profile of v8, /device:TPU:1, one launch (start us, length us, event | category | flops | bytes accessed | tf_op | source)
XLA Modules:
  0.0 63.9 jit_solution(133639282730639375)
XLA Ops:
  0.6 60.2 %splat.1 = (f32[3,4096]{1,0:T(4,128)}, f32[9,64,128]{2,1,0:T(8,128)}, f32[80,128]{1,0:T(8,128)}) custom-call(s32[16]{0:T(128)} %count_ref.1, s32[16]{0:T(128)} %order_ref.1, f32[3]{0:T(128)} %angle_ref.1, s32[16,512]{1,0:T(8,128)} %owner_hbm.1, s32[16,512]{1,0:T(8,128)} %local_hbm.1, f32[3,4096]{1,0:T(4,128)} %cot_hbm.1, f32[59,8192]{1,0:T(8,128)} %gauss_ref.1), custom_call_target="tpu_custom_call" | custom-call | tf_op jit(solution)/shard_map/splat/pallas_call | solution.py:654
  60.9 3.0 %pull.1 = (f32[59,8192]{1,0:T(8,128)}, f32[3,4096]{1,0:T(4,128)}) custom-call(f32[80,128]{1,0:T(8,128)} %get-tuple-element.7.view_ref, f32[59,8192]{1,0:T(8,128)} %gauss_ref.1, f32[9,64,128]{2,1,0:T(8,128)} %get-tuple-element.8.sum_ref, f32[3,4096]{1,0:T(4,128)} %get-tuple-element.9.shot_ref), custom_call_target="tpu_custom_call" | custom-call | tf_op jit(solution)/shard_map/pull/pallas_call | solution.py:702
